TPU v7x, 32 devices: a whole 2x2x4 slice. The times are simulated.
32 devices in a mesh: dp: 8 (over z, core), tensor: 4 (over y, x).
Axes of the slice: x: 2, y: 2, z: 4, core: 2. Of those that a mesh axis runs over, the one named last changes fastest.
Arguments:
- tokens: bfloat16 [24576, 1024], P('dp'), may hold values from -6 to 6
- lengths: int32 [24], P('dp'), may hold values from 512 to 1024, as said below
- routes: int32 [24576, 1], P('dp'), may hold values from 0 to 7
- fill_order: int32 [8, 3072], P('dp'), may hold values from 0 to 3071, each once within a row
- norm_gain: float32 [1024], replicated, may hold values from 0.1 to 1.9
- norm_bias: float32 [1024], replicated, may hold values from -3 to 3
- qkv_weight: bfloat16 [1024, 16, 192], P(None, 'tensor'), may hold values from -0.1875 to 0.1875
- out_weight: bfloat16 [16, 64, 1024], P('tensor'), may hold values from -0.75 to 0.75
- centroids: bfloat16 [8, 1024], P('dp'), may hold values from -0.125 to 0.125
- expert_in: bfloat16 [8, 2, 1024, 4096], P('dp', None, None, 'tensor'), may hold values from -0.1875 to 0.1875
- expert_out: bfloat16 [8, 2, 4096, 1024], P('dp', None, 'tensor'), may hold values from -0.09375 to 0.09375
- cotangent: bfloat16 [24576, 1024], P('dp'), may hold values from -6 to 6
Outputs:
- output: bfloat16 [24576, 1024], P('dp')
- grad_tokens: bfloat16 [24576, 1024], P('dp')
- grad_norm_gain: float32 [1024], P('tensor')
- grad_norm_bias: float32 [1024], P('tensor')
- grad_qkv_weight: float32 [1024, 16, 192], P(None, 'tensor')
- grad_out_weight: float32 [16, 64, 1024], P('tensor')
- grad_centroids: float32 [8, 1024], P('dp')
- grad_expert_in: float32 [8, 2, 1024, 4096], P('dp', None, None, 'tensor')
- grad_expert_out: float32 [8, 2, 4096, 1024], P('dp', None, 'tensor')
Inputs may be any that keep to these rules, and one draw needn't show every extreme that they name: `lengths`: valid tokens of each sequence; one sequence has exactly 1024 and one exactly 512.
All inputs are finite; a program needn't handle non-finite values.
Results may differ from a plain program's by a relative error of at most 0.015.
Values may be sent and summed in bfloat16 or wider, within the bound.
A program may use at most 448 MiB of HBM per device.

v0:
```python
import math
import jax
import jax.numpy as jnp
from jax import lax
from jax.sharding import PartitionSpec as P

EPSILON = 1e-05
HIGHEST = lax.Precision.HIGHEST
F32 = jnp.float32
BF16 = jnp.bfloat16


class Grid:

    def __init__(self, size):
        inner = int(math.isqrt(size))
        while size % inner:
            inner -= 1
        self.size = size
        self.parts = {"x": inner, "y": size // inner}

    def _pairs(self, axis, shift):
        wide, tall = (self.parts["x"], self.parts["y"])
        pairs = []
        for row in range(tall):
            for col in range(wide):
                if axis == "x":
                    other = row * wide + (col + shift) % wide
                else:
                    other = (row + shift) % tall * wide + col
                pairs.append((other, row * wide + col))
        return pairs

    def fetch(self, value, axis, shift=1):
        return lax.ppermute(value, "tensor", self._pairs(axis, shift))

    def gather_list(self, value, axis):
        return [value] + [self.fetch(value, axis, s) for s in range(1, self.parts[axis])]

    def scatter_list(self, parts, axis):
        total = parts[0]
        for s in range(1, self.parts[axis]):
            total = total + self.fetch(parts[s].astype(BF16), axis, -s).astype(F32)
        return total


def gather_rows(grid, value):
    if grid.size != 4:
        return lax.all_gather(value, "tensor", axis=0, tiled=False)
    half = value.shape[0] // 2
    me = lax.axis_index("tensor")
    first, second = (value[:half], value[half:])
    first_x = grid.fetch(first, "x")
    second_y = grid.fetch(second, "y")
    first_y = grid.fetch(first, "y")
    second_x = grid.fetch(second, "x")
    first_xy = grid.fetch(first_x, "y")
    second_xy = grid.fetch(second_y, "x")
    out = jnp.zeros((4,) + value.shape, value.dtype)
    out = lax.dynamic_update_slice(out, value[None], (me, 0, 0))
    for other, top, bottom in (
        (1, first_x, second_x),
        (2, first_y, second_y),
        (3, first_xy, second_xy),
    ):
        place = jnp.bitwise_xor(me, other)
        out = lax.dynamic_update_slice(out, top[None], (place, 0, 0))
        out = lax.dynamic_update_slice(out, bottom[None], (place, half, 0))
    return out


def scatter_rows(grid, term):
    size, rows, width = term.shape
    if size != 4:
        return lax.psum_scatter(
            term.astype(BF16), "tensor", scatter_dimension=0, tiled=False
        ).astype(F32)
    me = lax.axis_index("tensor")
    half = width // 2

    def pick(other, low):
        place = jnp.bitwise_xor(me, other)
        return lax.dynamic_slice(term, (place, 0, low), (1, rows, half))[0]

    totals = []
    for low, near, far, near_axis, far_axis in ((0, 1, 2, "x", "y"), (half, 2, 1, "y", "x")):
        got_far = grid.fetch(pick(3, low).astype(BF16), near_axis)
        got_own = grid.fetch(pick(near, low).astype(BF16), near_axis)
        onward = pick(far, low).astype(F32) + got_far.astype(F32)
        got = grid.fetch(onward.astype(BF16), far_axis)
        totals.append(pick(0, low).astype(F32) + got_own.astype(F32) + got.astype(F32))
    return jnp.concatenate(totals, axis=1)


def gelu_pair(pre):
    cdf = 0.5 * (1.0 + lax.erf(pre * 2.0 ** (-0.5)))
    density = jnp.exp(-0.5 * pre * pre) * (2.0 * math.pi) ** (-0.5)
    return ((pre * cdf).astype(BF16), (cdf + pre * density).astype(BF16))


def plan_slots(routes, order, lengths, seq_len, experts, capacity, padded):
    count = routes.shape[0]
    seq_count = lengths.shape[0]
    places = jnp.arange(count, dtype=jnp.int32)
    limits = jnp.broadcast_to(lengths[:, None], (seq_count, seq_len)).reshape(count)
    is_valid = places % seq_len < limits
    order_row = order.reshape(count)
    route_sorted = routes.reshape(count)[order_row]
    valid_sorted = is_valid[order_row]
    matches = (
        (route_sorted[:, None] == jnp.arange(experts, dtype=jnp.int32)[None, :])
        & valid_sorted[:, None]
    ).astype(jnp.int32)
    before = jnp.cumsum(matches, axis=0) - matches
    rank_sorted = jnp.sum(before * matches, axis=1)
    kept_sorted = valid_sorted & (rank_sorted < capacity)
    slot_sorted = jnp.where(kept_sorted, route_sorted * padded + rank_sorted, experts * padded)
    slot_token = (
        jnp.full((experts * padded + 1,), count, jnp.int32)
        .at[slot_sorted]
        .set(order_row)[: experts * padded]
    )
    token_slot = jnp.zeros((count,), jnp.int32).at[order_row].set(slot_sorted)
    return (slot_token, token_slot)


def dot(a, b, contract):
    return lax.dot_general(a, b, (contract, ((), ())), preferred_element_type=F32)


def body(
    tokens,
    lengths,
    routes,
    fill_order,
    norm_gain,
    norm_bias,
    qkv_weight,
    out_weight,
    centroids,
    expert_in,
    expert_out,
    cotangent,
):
    tok_count, model_width = tokens.shape
    seq_count = lengths.shape[0]
    seq_len = tok_count // seq_count
    heads_here = qkv_weight.shape[1]
    head_size = out_weight.shape[1]
    experts = lax.axis_size("dp")
    shards = lax.axis_size("tensor")
    grid = Grid(shards)
    me = lax.axis_index("tensor")
    capacity = (9 * tok_count + 8 * experts - 1) // (8 * experts)
    share = 16 * -(-capacity // (16 * shards))
    padded = share * shards
    own_rows = experts * share
    tok_rows = tok_count // shards
    score_scale = head_size ** (-0.5)
    row_axis = ("y", "x")
    weight_axis = ("x", "y")
    win = [grid.gather_list(expert_in[0, k], weight_axis[k]) for k in range(2)]
    wout = [grid.gather_list(expert_out[0, k], weight_axis[k]) for k in range(2)]
    out_flat = out_weight.reshape(heads_here * head_size, model_width)
    out_all = lax.all_gather(out_flat, "tensor", axis=0, tiled=True)
    slot_token, token_slot = plan_slots(
        routes, fill_order, lengths, seq_len, experts, capacity, padded
    )
    own_slot = lax.dynamic_slice_in_dim(
        slot_token.reshape(experts, padded), me * share, share, 1
    ).reshape(own_rows)
    own_filled = (own_slot < tok_count)[:, None]
    own_index = jnp.minimum(own_slot, tok_count - 1)
    kept = (token_slot < experts * padded)[:, None]
    tok_expert = jnp.minimum(token_slot // padded, experts - 1)
    tok_rank = token_slot % padded
    tok_place = (tok_rank // share * experts + tok_expert) * share + tok_rank % share

    def to_experts(rows):
        picked = jnp.where(own_filled, rows[own_index], jnp.zeros((), rows.dtype))
        moved = lax.all_to_all(
            picked.reshape(experts, share, model_width),
            "dp",
            split_axis=0,
            concat_axis=0,
            tiled=True,
        )
        return moved.reshape(own_rows, model_width)

    def from_experts(rows):
        moved = lax.all_to_all(
            rows.reshape(experts, share, model_width), "dp", split_axis=0, concat_axis=0, tiled=True
        )
        every = gather_rows(grid, moved.reshape(own_rows, model_width))
        picked = every.reshape(shards * own_rows, model_width)[tok_place]
        return jnp.where(kept, picked, jnp.zeros((), rows.dtype)).astype(F32)

    grad_ret = to_experts(cotangent).astype(F32)
    input_rows = tokens.astype(F32)
    centre = input_rows - jnp.mean(input_rows, axis=1, keepdims=True)
    inverse_scale = lax.rsqrt(jnp.mean(centre * centre, axis=1, keepdims=True) + EPSILON)
    normed = centre * inverse_scale
    ln_in = (normed * norm_gain + norm_bias).astype(BF16)
    projected = jnp.einsum("td,dhe->the", ln_in, qkv_weight, preferred_element_type=F32).astype(
        BF16
    )
    projected = projected.reshape(seq_count, seq_len, heads_here, 3 * head_size)
    queries = projected[..., :head_size]
    key_vectors = projected[..., head_size : 2 * head_size]
    values = projected[..., 2 * head_size :]
    positions = jnp.arange(seq_len, dtype=jnp.int32)
    allowed = (positions[None, None, :] <= positions[None, :, None]) & (
        positions[None, None, :] < lengths[:, None, None]
    )

    def attention_probs(log_total):
        scores = (
            jnp.einsum("sqhd,skhd->shqk", queries, key_vectors, preferred_element_type=F32)
            * score_scale
        )
        scores = jnp.where(allowed[:, None], scores, -1e30)
        if log_total is None:
            row_max = jnp.max(scores, axis=-1, keepdims=True)
            log_total = row_max + jnp.log(
                jnp.sum(jnp.exp(scores - row_max), axis=-1, keepdims=True)
            )
        return (jnp.exp(scores - log_total), log_total)

    attention_weights, log_total = attention_probs(None)
    attended = jnp.einsum(
        "shqk,skhd->sqhd", attention_weights.astype(BF16), values, preferred_element_type=F32
    ).astype(BF16)
    attended = attended.reshape(tok_count, heads_here * head_size)
    every_attended = gather_rows(grid, attended)
    attended_all = jnp.swapaxes(every_attended, 0, 1).reshape(tok_count, -1)
    mixed = input_rows + dot(attended_all, out_all, ((1,), (0,)))
    sent = mixed.astype(BF16)
    expert_rows = to_experts(sent)
    centroid = centroids[0]
    gate = jax.nn.sigmoid(jnp.dot(expert_rows, centroid, preferred_element_type=F32))[:, None]
    current = expert_rows.astype(F32)
    saved = []
    for k in range(2):
        rows_in = jnp.concatenate(grid.gather_list(current.astype(BF16), row_axis[k]), axis=0)
        acts, slopes = ([], [])
        total = None
        for w_in, w_out in zip(win[k], wout[k]):
            act, slope = gelu_pair(dot(rows_in, w_in, ((1,), (0,))))
            term = dot(act, w_out, ((1,), (0,)))
            total = term if total is None else total + term
            acts.append(act)
            slopes.append(slope)
        parts = jnp.split(total, grid.parts[row_axis[k]], axis=0)
        current = current + grid.scatter_list(parts, row_axis[k])
        saved.append((rows_in, acts, slopes))
    output = (mixed + from_experts((gate * current).astype(BF16))).astype(BF16)
    grad_gate = jnp.sum(grad_ret * current, axis=1, keepdims=True)
    grad_logit = grad_gate * gate * (1.0 - gate)
    grad_current = gate * grad_ret
    grads_in = [None, None]
    grads_back = [None, None]
    for k in (1, 0):
        rows_in, acts, slopes = saved[k]
        branch = jnp.concatenate(grid.gather_list(grad_current.astype(BF16), row_axis[k]), axis=0)
        total = None
        in_parts, out_parts = ([], [])
        for w_in, w_out, act, slope in zip(win[k], wout[k], acts, slopes):
            grad_pre = (dot(branch, w_out, ((1,), (1,))) * slope.astype(F32)).astype(BF16)
            term = dot(grad_pre, w_in, ((1,), (1,)))
            total = term if total is None else total + term
            out_parts.append(dot(act, branch, ((0,), (0,))))
            in_parts.append(dot(rows_in, grad_pre, ((0,), (0,))))
        parts = jnp.split(total, grid.parts[row_axis[k]], axis=0)
        grad_current = grad_current + grid.scatter_list(parts, row_axis[k])
        grads_in[k] = grid.scatter_list(in_parts, weight_axis[k])
        grads_back[k] = grid.scatter_list(out_parts, weight_axis[k])
    grad_rows = (grad_current + grad_logit * centroid.astype(F32)[None, :]).astype(BF16)
    grad_centroid = lax.psum(
        jnp.sum(grad_logit * expert_rows.astype(F32), axis=0, keepdims=True), "tensor"
    )
    grad_mixed = cotangent.astype(F32) + from_experts(grad_rows)
    grad_attn = grad_mixed.astype(BF16)
    grad_out_local = dot(attended, grad_attn, ((0,), (0,))).reshape(
        heads_here, head_size, model_width
    )
    grad_attended = dot(grad_attn, out_flat, ((1,), (1,))).astype(BF16)
    grad_attended = grad_attended.reshape(seq_count, seq_len, heads_here, head_size)
    attention_weights, unused_total = attention_probs(log_total)
    grad_probs = jnp.einsum("sqhd,skhd->shqk", grad_attended, values, preferred_element_type=F32)
    row_delta = jnp.sum(attention_weights * grad_probs, axis=-1, keepdims=True)
    grad_scores = (attention_weights * (grad_probs - row_delta)).astype(BF16)
    grad_query = (
        jnp.einsum("shqk,skhd->sqhd", grad_scores, key_vectors, preferred_element_type=F32)
        * score_scale
    ).astype(BF16)
    grad_key = (
        jnp.einsum("shqk,sqhd->skhd", grad_scores, queries, preferred_element_type=F32)
        * score_scale
    ).astype(BF16)
    grad_value = jnp.einsum(
        "shqk,sqhd->skhd", attention_weights.astype(BF16), grad_attended, preferred_element_type=F32
    ).astype(BF16)
    grad_projected = jnp.concatenate([grad_query, grad_key, grad_value], axis=-1).reshape(
        tok_count, heads_here, 3 * head_size
    )
    grad_qkv_local = jnp.einsum("td,the->dhe", ln_in, grad_projected, preferred_element_type=F32)
    grad_ln_part = jnp.einsum("the,dhe->td", grad_projected, qkv_weight, preferred_element_type=F32)
    grad_ln = scatter_rows(grid, grad_ln_part.astype(BF16).reshape(shards, tok_rows, model_width))

    def own(rows):
        return lax.dynamic_slice_in_dim(rows, me * tok_rows, tok_rows, 0)

    own_scale = own(inverse_scale)
    own_normed = own(centre) * own_scale
    grad_normed = grad_ln * norm_gain
    mean_plain = jnp.mean(grad_normed, axis=1, keepdims=True)
    mean_cross = jnp.mean(grad_normed * own_normed, axis=1, keepdims=True)
    grad_input = own(grad_mixed) + own_scale * (grad_normed - mean_plain - own_normed * mean_cross)
    grad_tokens = gather_rows(grid, grad_input.astype(BF16)).reshape(tok_count, model_width)
    norm_parts = jnp.stack([jnp.sum(grad_ln * own_normed, axis=0), jnp.sum(grad_ln, axis=0)])
    norm_total = lax.dynamic_slice_in_dim(
        lax.psum(norm_parts, ("dp", "tensor")),
        me * (model_width // shards),
        model_width // shards,
        1,
    )
    grad_qkv_weight, grad_out_weight = lax.psum((grad_qkv_local, grad_out_local), "dp")
    return (
        output,
        grad_tokens,
        norm_total[0],
        norm_total[1],
        grad_qkv_weight,
        grad_out_weight,
        grad_centroid,
        jnp.stack(grads_in)[None],
        jnp.stack(grads_back)[None],
    )


def solution(mesh):
    return jax.shard_map(
        body,
        mesh=mesh,
        in_specs=(
            P("dp", None),
            P("dp"),
            P("dp", None),
            P("dp", None),
            P(),
            P(),
            P(None, "tensor", None),
            P("tensor", None, None),
            P("dp", None),
            P("dp", None, None, "tensor"),
            P("dp", None, "tensor", None),
            P("dp", None),
        ),
        out_specs=(
            P("dp", None),
            P("dp", None),
            P("tensor"),
            P("tensor"),
            P(None, "tensor", None),
            P("tensor", None, None),
            P("dp", None),
            P("dp", None, None, "tensor"),
            P("dp", None, "tensor", None),
        ),
        check_vma=False,
    )
```

profile of v0, /device:TPU:0, one launch (start us, length us, event | category | flops | bytes accessed | tf_op | source)
XLA Modules:
  0.0 1408.5 jit_solution(3828291646385503996)
XLA Ops:
  25.6 13.7 reshape.318
  46.0 19.2 %fusion = (f32[3,4,1024]{2,1,0:T(4,128)S(1)}, f32[3,4,1024,1024]{2,3,1,0:T(8,128)}) fusion(pred[3,1024,1024]{1,2,0:T(8,128)(4,1)S(1)} %broadcast_and_fusion, bf16[3,1024,4,64]{1,0,3,2:T(4,128)(2,1)S(1)} %get-tuple-element.29, bf16[3,1024,4,64]{1,0,3,2:T(4,128)(2,1)S(1)} %get-tuple-element.27), kind=kOutput, calls=%fused_computation.13 | convolution fusion | flops 1648349184 | bytes 56672256 | tf_op jit(solution)/shard_map/sqhd,skhd->shqk/dot_general | solution.py:218
  65.2 21.3 %exponential_reduce_fusion = f32[3,4,1024]{2,1,0:T(4,128)S(1)} fusion(f32[3,4,1024,1024]{2,3,1,0:T(8,128)} %get-tuple-element.54, f32[3,4,1024]{2,1,0:T(4,128)S(1)} %get-tuple-element.53, pred[3,1024,1024]{1,2,0:T(8,128)(4,1)S(1)} %broadcast_and_fusion), kind=kLoop, calls=%fused_computation.11 | loop fusion | flops 50319360 | bytes 53575680 | tf_op jit(solution)/shard_map/reduce_sum | solution.py:225
  86.6 20.1 %fusion.39 = bf16[3,1024,4,64]{1,3,2,0:T(8,128)(2,1)S(1)} fusion(bf16[3,1024,4,64]{1,0,3,2:T(4,128)(2,1)S(1)} %get-tuple-element.28, f32[3,4,1024,1024]{2,3,1,0:T(8,128)} %get-tuple-element.54, f32[3,4,1024]{2,1,0:T(4,128)S(1)} %log_add_fusion, pred[3,1024,1024]{1,2,0:T(8,128)(4,1)S(1)} %broadcast_and_fusion), kind=kOutput, calls=%fused_computation.133 | convolution fusion | flops 1661730816 | bytes 56672256 | tf_op jit(solution)/shard_map/shqk,skhd->sqhd/dot_general | solution.py:230
  120.9 19.4 %gather_fusion = pred[3072]{0:T(1024)(128)(4,1)S(1)} fusion(pred[3072]{0:T(1024)(128)(4,1)S(1)} %fusion.60, s32[3072]{0:T(1024)S(1)} %broadcast_clamp_fusion), kind=kCustom, calls=%fused_computation | custom fusion | bytes 18432 | tf_op jit(solution)/shard_map/gather | solution.py:109
  140.3 17.4 %gather_fusion.1 = s32[3072]{0:T(1024)S(1)} fusion(s32[3072]{0:T(1024)S(1)} %bitcast.249, s32[3072]{0:T(1024)S(1)} %broadcast_clamp_fusion), kind=kCustom, calls=%fused_computation.1 | custom fusion | bytes 36864 | tf_op jit(solution)/shard_map/gather | solution.py:108
  160.7 11.8 scatter_custom_fusion.1
  177.5 8.8 gather_fusion.4
  198.2 6.9 collective-permute-done.4
  207.4 14.0 fusion.2
  221.4 9.1 gather_fusion.2
  245.4 37.3 %all-to-all-done = bf16[8,112,1024]{2,1,0:T(8,128)(2,1)S(1)} async-done(((bf16[8,112,1024]{2,1,0:T(8,128)(2,1)}), bf16[8,112,1024]{2,1,0:T(8,128)(2,1)S(1)}, u32[]{:S(2)}, u32[]{:S(2)}) %all-to-all-start) | async-done | bytes 1835040 | tf_op jit(solution)/shard_map/all_to_all | solution.py:181
  292.6 31.6 %collective-permute-done.6 = bf16[896,1024]{1,0:T(8,128)(2,1)S(1)} collective-permute-done((bf16[896,1024]{1,0:T(8,128)(2,1)S(1)}, bf16[896,1024]{1,0:T(8,128)(2,1)S(1)}, u32[]{:S(2)}, u32[]{:S(2)}) %collective-permute-start.6) | collective-permute-done | bytes 1835040 | tf_op jit(solution)/shard_map/ppermute | solution.py:35
  324.2 10.0 multiply_convert_fusion.7
  334.2 8.3 multiply_convert_fusion.8
  362.3 36.4 %collective-permute-done.9 = bf16[896,1024]{1,0:T(8,128)(2,1)} collective-permute-done((bf16[896,1024]{1,0:T(8,128)(2,1)}, bf16[896,1024]{1,0:T(8,128)(2,1)}, u32[]{:S(2)}, u32[]{:S(2)}) %collective-permute-start.9) | collective-permute-done | bytes 1835040 | tf_op jit(solution)/shard_map/ppermute | solution.py:35
  409.3 34.3 %collective-permute-done.11 = bf16[1024,1024]{1,0:T(8,128)(2,1)} collective-permute-done((bf16[1024,1024]{1,0:T(8,128)(2,1)}, bf16[1024,1024]{1,0:T(8,128)(2,1)}, u32[]{:S(2)}, u32[]{:S(2)}) %collective-permute-start.11) | collective-permute-done | bytes 2097184 | tf_op jit(solution)/shard_map/ppermute | solution.py:35
  446.8 9.2 multiply_convert_fusion.5
  456.0 9.0 multiply_convert_fusion.6
  465.0 15.5 %collective-permute-done.20 = bf16[896,1024]{1,0:T(8,128)(2,1)S(1)} collective-permute-done((bf16[896,1024]{1,0:T(8,128)(2,1)S(1)}, bf16[896,1024]{1,0:T(8,128)(2,1)S(1)}, u32[]{:S(2)}, u32[]{:S(2)}) %collective-permute-start.20) | collective-permute-done | bytes 1835040 | tf_op jit(solution)/shard_map/ppermute | solution.py:35
  480.5 10.3 multiply_convert_fusion.4
  498.2 9.9 multiply_convert_fusion.3
  508.1 8.4 convolution_add_fusion.1
  518.4 8.7 fusion.87
  527.1 9.3 convolution_add_fusion.2
  540.4 19.4 %collective-permute-done.21 = bf16[896,1024]{1,0:T(8,128)(2,1)S(1)} collective-permute-done((bf16[896,1024]{1,0:T(8,128)(2,1)S(1)}, bf16[896,1024]{1,0:T(8,128)(2,1)S(1)}, u32[]{:S(2)}, u32[]{:S(2)}) %collective-permute-start.21) | collective-permute-done | bytes 1835040 | tf_op jit(solution)/shard_map/ppermute | solution.py:35
  559.8 33.0 %collective-permute-done.13 = bf16[896,1024]{1,0:T(8,128)(2,1)} collective-permute-done((bf16[896,1024]{1,0:T(8,128)(2,1)S(1)}, bf16[896,1024]{1,0:T(8,128)(2,1)}, u32[]{:S(2)}, u32[]{:S(2)}) %collective-permute-start.13) | collective-permute-done | bytes 1835040 | tf_op jit(solution)/shard_map/ppermute | solution.py:35
  600.3 34.3 %collective-permute-done.22 = bf16[896,1024]{1,0:T(8,128)(2,1)S(1)} collective-permute-done((bf16[896,1024]{1,0:T(8,128)(2,1)S(1)}, bf16[896,1024]{1,0:T(8,128)(2,1)S(1)}, u32[]{:S(2)}, u32[]{:S(2)}) %collective-permute-start.22) | collective-permute-done | bytes 1835040 | tf_op jit(solution)/shard_map/ppermute | solution.py:35
  634.5 10.6 multiply_convert_fusion.2
  649.3 9.7 multiply_convert_fusion.1
  659.0 7.0 convolution_add_fusion
  672.0 33.6 %collective-permute-done.23 = bf16[896,1024]{1,0:T(8,128)(2,1)} collective-permute-done((bf16[896,1024]{1,0:T(8,128)(2,1)}, bf16[896,1024]{1,0:T(8,128)(2,1)}, u32[]{:S(2)}, u32[]{:S(2)}) %collective-permute-start.23) | collective-permute-done | bytes 1835040 | tf_op jit(solution)/shard_map/ppermute | solution.py:35
  705.6 8.3 fusion.30
  713.9 7.4 all-to-all-start.1
  721.3 8.6 convolution_convert_fusion.1
  731.3 7.3 convolution_convert_fusion.3
  739.3 11.9 scatter_custom_fusion
  753.2 10.5 psum.31
  769.2 9.7 collective-permute-done.45
  778.9 9.8 add_bitcast_fusion
  788.7 34.7 %collective-permute-done.43 = bf16[1024,1024]{1,0:T(8,128)(2,1)} collective-permute-done((bf16[1024,1024]{1,0:T(8,128)(2,1)}, bf16[1024,1024]{1,0:T(8,128)(2,1)}, u32[]{:S(2)}, u32[]{:S(2)}) %collective-permute-start.43) | collective-permute-done | bytes 2097184 | tf_op jit(solution)/shard_map/ppermute | solution.py:35
  823.4 8.2 add_bitcast_fusion.2
  869.3 13.7 collective-permute-done.15
  892.7 9.8 collective-permute-done.24
  904.9 17.3 %collective-permute-done.25 = bf16[448,1024]{1,0:T(8,128)(2,1)S(1)} collective-permute-done((bf16[448,1024]{1,0:T(8,128)(2,1)S(1)}, bf16[448,1024]{1,0:T(8,128)(2,1)S(1)}, u32[]{:S(2)}, u32[]{:S(2)}) %collective-permute-start.25) | collective-permute-done | bytes 917536 | tf_op jit(solution)/shard_map/ppermute | solution.py:35
  933.0 16.1 %collective-permute-done.18 = bf16[448,1024]{1,0:T(8,128)(2,1)S(1)} collective-permute-done((bf16[448,1024]{1,0:T(8,128)(2,1)}, bf16[448,1024]{1,0:T(8,128)(2,1)S(1)}, u32[]{:S(2)}, u32[]{:S(2)}) %collective-permute-start.18) | collective-permute-done | bytes 917536 | tf_op jit(solution)/shard_map/ppermute | solution.py:35
  951.7 15.2 %collective-permute-done.28 = bf16[448,1024]{1,0:T(8,128)(2,1)S(1)} collective-permute-done((bf16[448,1024]{1,0:T(8,128)(2,1)S(1)}, bf16[448,1024]{1,0:T(8,128)(2,1)S(1)}, u32[]{:S(2)}, u32[]{:S(2)}) %collective-permute-start.28) | collective-permute-done | bytes 917536 | tf_op jit(solution)/shard_map/ppermute | solution.py:35
  967.9 18.9 %collective-permute-done.19 = bf16[448,1024]{1,0:T(8,128)(2,1)S(1)} collective-permute-done((bf16[448,1024]{1,0:T(8,128)(2,1)S(1)}, bf16[448,1024]{1,0:T(8,128)(2,1)S(1)}, u32[]{:S(2)}, u32[]{:S(2)}) %collective-permute-start.19) | collective-permute-done | bytes 917536 | tf_op jit(solution)/shard_map/ppermute | solution.py:35
  986.8 19.7 %collective-permute-done.29 = bf16[448,1024]{1,0:T(8,128)(2,1)S(1)} collective-permute-done((bf16[448,1024]{1,0:T(8,128)(2,1)S(1)}, bf16[448,1024]{1,0:T(8,128)(2,1)S(1)}, u32[]{:S(2)}, u32[]{:S(2)}) %collective-permute-start.29) | collective-permute-done | bytes 917536 | tf_op jit(solution)/shard_map/ppermute | solution.py:35
  1007.8 19.9 %gather_fusion.3 = bf16[3072,1024]{1,0:T(8,128)(2,1)} fusion(bf16[3584,1024]{1,0:T(8,128)(2,1)} %bitcast.37, s32[3072]{0:T(1024)S(1)} %fusion.66), kind=kCustom, calls=%fused_computation.3 | custom fusion | bytes 12595200 | tf_op jit(solution)/shard_map/gather | solution.py:195
  1027.7 19.9 %gather_fusion.5 = bf16[3072,1024]{1,0:T(8,128)(2,1)} fusion(bf16[3584,1024]{1,0:T(8,128)(2,1)} %bitcast.51, s32[3072]{0:T(1024)S(1)} %fusion.66), kind=kCustom, calls=%fused_computation.5 | custom fusion | bytes 12595200 | tf_op jit(solution)/shard_map/gather | solution.py:195
  1047.6 17.5 %convert_add_fusion.1 = (f32[3072,1024]{1,0:T(8,128)S(1)}, bf16[3072,1024]{1,0:T(8,128)(2,1)}) fusion(bf16[3072,1024]{1,0:T(8,128)(2,1)} %param.23, bf16[3072,1024]{1,0:T(8,128)(2,1)} %gather_fusion.5, pred[3072]{0:T(1024)(128)(4,1)S(1)} %broadcast_compare_fusion, bf16[3072,1024]{1,0:T(8,128)(2,1)} %gather_fusion.3, f32[3072,1024]{1,0:T(8,128)} %get-tuple-element.56, ...), kind=kLoop, calls=%fused_computation.19 | loop fusion | flops 31457280 | bytes 56626176 | tf_op jit(solution)/shard_map/add | solution.py:281
  1078.7 36.9 %multiply_reduce_fusion = (f32[3,4,1024]{2,1,0:T(4,128)S(1)}, f32[3,4,1024,1024]{2,3,1,0:T(8,128)}) fusion(f32[3,4,1024,1024]{2,3,1,0:T(8,128)} %get-tuple-element.54, f32[3,4,1024]{2,1,0:T(4,128)S(1)} %copy-done.33, pred[3,1024,1024]{1,2,0:T(8,128)(4,1)} %copy-done.3, bf16[3,1024,4,64]{1,3,2,0:T(8,128)(2,1)S(1)} %copy.37, ...), kind=kOutput, calls=%fused_computation.9 | convolution fusion | flops 1673515008 | bytes 107053056 | tf_op jit(solution)/shard_map/sqhd,skhd->shqk/dot_general | solution.py:289
  1115.6 42.3 %multiply_convert_fusion = bf16[3,4,1024,1024]{2,3,1,0:T(8,128)(2,1)} fusion(f32[3,4,1024,1024]{2,3,1,0:T(8,128)} %get-tuple-element.66, f32[3,4,1024,1024]{2,3,1,0:T(8,128)} %get-tuple-element.54, f32[3,4,1024]{2,1,0:T(4,128)S(1)} %get-tuple-element.65, f32[3,4,1024]{2,1,0:T(4,128)S(1)} %copy-done.33, pred[3,1024,1024]{1,2,0:T(8,128)(4,1)} %copy-done.3), kind=kLoop, calls=%fused_computation.8 | loop fusion | flops 75497472 | bytes 129073152 | tf_op jit(solution)/shard_map/convert_element_type | solution.py:291
  1157.9 13.4 fusion.41
  1171.3 14.0 fusion.42
  1185.4 20.3 %fusion.40 = bf16[3,1024,4,64]{1,3,2,0:T(8,128)(2,1)S(1)} fusion(bf16[3,1024,4,64]{1,3,2,0:T(8,128)(2,1)} %copy-done.12, f32[3,4,1024,1024]{2,3,1,0:T(8,128)} %get-tuple-element.54, f32[3,4,1024]{2,1,0:T(4,128)S(1)} %copy-done.33, pred[3,1024,1024]{1,2,0:T(8,128)(4,1)} %copy-done.3), kind=kOutput, calls=%fused_computation.134 | convolution fusion | flops 1661730816 | bytes 56672256 | tf_op jit(solution)/shard_map/shqk,sqhd->skhd/dot_general | solution.py:300
  1237.3 9.3 add_bitcast_fusion.3
  1259.3 9.3 collective-permute-done.32
  1272.1 7.0 fusion.90
  1300.2 8.5 maximum_bitcast_fusion
  1308.7 49.7 %psum.28 = f32[2,1024]{1,0:T(2,128)S(1)} all-reduce(f32[2,1024]{1,0:T(2,128)S(1)} %pad_maximum_fusion.6), channel_id=1, replica_groups=mesh['dp'=8,'tensor'=4] {'dp','tensor'}, use_global_device_ids=true, to_apply=%region_15.16 | all-reduce | flops 2048 | bytes 16384 | tf_op jit(solution)/shard_map/psum | solution.py:322
  1367.9 10.0 collective-permute-done.40
  1379.8 16.4 %all-reduce.3.cloned.1.call-done = (f32[1024,4,192]{0,2,1:T(8,128)}, f32[4,64,1024]{2,1,0:T(8,128)}) async-done(((f32[1024,4,192]{0,2,1:T(8,128)}, f32[4,64,1024]{2,1,0:T(8,128)}), (f32[1024,4,192]{0,2,1:T(8,128)}, f32[4,64,1024]{2,1,0:T(8,128)})) %all-reduce.3.cloned.1.call-update) | async-done | bytes 4194320 | tf_op jit(solution)/shard_map/psum | solution.py:327
  (356 shorter events, 323.7 us)
Async XLA Ops:
  7.2 200.2 %all-gather.2.cloned.1.call-start = ((), (), s32[]{:S(2)}) async-start(), calls=%async_computation.4 | async-start | bytes 2621440 | tf_op jit(solution)/shard_map/all_gather | solution.py:165
  110.7 75.7 %collective-permute-start = (bf16[1536,256]{0,1:T(8,128)(2,1)}, bf16[1536,256]{0,1:T(8,128)(2,1)}, u32[]{:S(2)}, u32[]{:S(2)}) collective-permute-start(bf16[1536,256]{0,1:T(8,128)(2,1)} %get-tuple-element.44), channel_id=1, source_target_pairs={{1,0},{0,1},{3,2},{2,3},{5,4},{4,5},{7,6},{6,7},{9,8},{8,9},{11,10... | collective-permute-start | bytes 2359304 | tf_op jit(solution)/shard_map/ppermute | solution.py:35
  113.6 80.4 %collective-permute-start.2 = (bf16[1536,256]{0,1:T(8,128)(2,1)}, bf16[1536,256]{0,1:T(8,128)(2,1)}, u32[]{:S(2)}, u32[]{:S(2)}) collective-permute-start(bf16[1536,256]{0,1:T(8,128)(2,1)} %get-tuple-element.44), channel_id=1, source_target_pairs={{2,0},{3,1},{0,2},{1,3},{6,4},{7,5},{4,6},{5,7},{10,8},{11,9},{8,1... | collective-permute-start | bytes 2359304 | tf_op jit(solution)/shard_map/ppermute | solution.py:35
  115.1 76.8 %collective-permute-start.1 = (bf16[1536,256]{0,1:T(8,128)(2,1)}, bf16[1536,256]{0,1:T(8,128)(2,1)}, u32[]{:S(2)}, u32[]{:S(2)}) collective-permute-start(bf16[1536,256]{0,1:T(8,128)(2,1)} %get-tuple-element.43), channel_id=1, source_target_pairs={{1,0},{0,1},{3,2},{2,3},{5,4},{4,5},{7,6},{6,7},{9,8},{8,9},{11,10... | collective-permute-start | bytes 2359304 | tf_op jit(solution)/shard_map/ppermute | solution.py:35
  115.7 72.7 %collective-permute-start.3 = (bf16[1536,256]{0,1:T(8,128)(2,1)}, bf16[1536,256]{0,1:T(8,128)(2,1)}, u32[]{:S(2)}, u32[]{:S(2)}) collective-permute-start(bf16[1536,256]{0,1:T(8,128)(2,1)} %get-tuple-element.43), channel_id=1, source_target_pairs={{2,0},{3,1},{0,2},{1,3},{6,4},{7,5},{4,6},{5,7},{10,8},{11,9},{8,1... | collective-permute-start | bytes 2359304 | tf_op jit(solution)/shard_map/ppermute | solution.py:35
  186.4 18.7 %collective-permute-start.4 = (bf16[1536,256]{0,1:T(8,128)(2,1)}, bf16[1536,256]{0,1:T(8,128)(2,1)S(1)}, u32[]{:S(2)}, u32[]{:S(2)}) collective-permute-start(bf16[1536,256]{0,1:T(8,128)(2,1)} %collective-permute-done), channel_id=1, source_target_pairs={{2,0},{3,1},{0,2},{1,3},{6,4},{7,5},{4,6},{5,7},{10,8},{11,9},{8,1... | collective-permute-start | bytes 2359304 | tf_op jit(solution)/shard_map/ppermute | solution.py:35
  188.4 18.1 %collective-permute-start.5 = (bf16[1536,256]{0,1:T(8,128)(2,1)}, bf16[1536,256]{0,1:T(8,128)(2,1)S(1)}, u32[]{:S(2)}, u32[]{:S(2)}) collective-permute-start(bf16[1536,256]{0,1:T(8,128)(2,1)} %collective-permute-done.3), channel_id=1, source_target_pairs={{1,0},{0,1},{3,2},{2,3},{5,4},{4,5},{7,6},{6,7},{9,8},{8,9},{11,10... | collective-permute-start | bytes 2359304 | tf_op jit(solution)/shard_map/ppermute | solution.py:35
  234.3 48.3 %all-to-all-start = ((bf16[8,112,1024]{2,1,0:T(8,128)(2,1)}), bf16[8,112,1024]{2,1,0:T(8,128)(2,1)S(1)}, u32[]{:S(2)}, u32[]{:S(2)}) async-start(bf16[8,112,1024]{2,1,0:T(8,128)(2,1)} %get-tuple-element.51), calls=%async_computation | async-start | bytes 3670016 | tf_op jit(solution)/shard_map/all_to_all | solution.py:181
  243.9 48.7 %collective-permute-start.7 = (bf16[1024,1024]{1,0:T(8,128)(2,1)}, bf16[1024,1024]{1,0:T(8,128)(2,1)}, u32[]{:S(2)}, u32[]{:S(2)}) collective-permute-start(bf16[1024,1024]{1,0:T(8,128)(2,1)} %get-tuple-element.35), channel_id=1, source_target_pairs={{1,0},{0,1},{3,2},{2,3},{5,4},{4,5},{7,6},{6,7},{9,8},{8,9},{11,10... | collective-permute-start | bytes 6291464 | tf_op jit(solution)/shard_map/ppermute | solution.py:35
  282.7 559.1 %copy-start.5 = (bf16[8,112,1024]{2,1,0:T(8,128)(2,1)}, bf16[8,112,1024]{2,1,0:T(8,128)(2,1)S(1)}, u32[]{:S(2)}) copy-start(bf16[8,112,1024]{2,1,0:T(8,128)(2,1)S(1)} %all-to-all-done) | copy-start | bytes 5505028
  282.7 41.6 %collective-permute-start.6 = (bf16[896,1024]{1,0:T(8,128)(2,1)S(1)}, bf16[896,1024]{1,0:T(8,128)(2,1)S(1)}, u32[]{:S(2)}, u32[]{:S(2)}) collective-permute-start(bf16[896,1024]{1,0:T(8,128)(2,1)S(1)} %bitcast.254), channel_id=1, source_target_pairs={{2,0},{3,1},{0,2},{1,3},{6,4},{7,5},{4,6},{5,7},{10,8},{11,9},{8,1... | collective-permute-start | bytes 5505032 | tf_op jit(solution)/shard_map/ppermute | solution.py:35
  287.9 46.4 %copy-start.23 = (bf16[1,2,1024,1024]{3,2,1,0:T(8,128)(2,1)S(1)}, bf16[1,2,1024,1024]{3,2,1,0:T(8,128)(2,1)}, u32[]{:S(2)}) copy-start(bf16[1,2,1024,1024]{3,2,1,0:T(8,128)(2,1)} %param.21) | copy-start | bytes 12582916
  287.9 58.7 %collective-permute-start.8 = (bf16[1024,1024]{1,0:T(8,128)(2,1)S(1)}, bf16[1024,1024]{1,0:T(8,128)(2,1)S(1)}, u32[]{:S(2)}, u32[]{:S(2)}) collective-permute-start(bf16[1024,1024]{1,0:T(8,128)(2,1)S(1)} %get-tuple-element.33), channel_id=1, source_target_pairs={{1,0},{0,1},{3,2},{2,3},{5,4},{4,5},{7,6},{6,7},{9,8},{8,9},{11,10... | collective-permute-start | bytes 6291464 | tf_op jit(solution)/shard_map/ppermute | solution.py:35
  355.4 43.3 %collective-permute-start.9 = (bf16[896,1024]{1,0:T(8,128)(2,1)}, bf16[896,1024]{1,0:T(8,128)(2,1)}, u32[]{:S(2)}, u32[]{:S(2)}) collective-permute-start(bf16[896,1024]{1,0:T(8,128)(2,1)} %split.75), channel_id=1, source_target_pairs={{2,0},{3,1},{0,2},{1,3},{6,4},{7,5},{4,6},{5,7},{10,8},{11,9},{8,1... | collective-permute-start | bytes 5505032 | tf_op jit(solution)/shard_map/ppermute | solution.py:35
  356.6 49.0 %all-to-all-start.2 = ((bf16[8,112,1024]{2,1,0:T(8,128)(2,1)}), bf16[8,112,1024]{2,1,0:T(8,128)(2,1)}, u32[]{:S(2)}, u32[]{:S(2)}) async-start(bf16[8,112,1024]{2,1,0:T(8,128)(2,1)} %get-tuple-element.52), calls=%async_computation.2 | async-start | bytes 3670016 | tf_op jit(solution)/shard_map/all_to_all | solution.py:181
  361.4 43.7 %copy-start.44 = (bf16[1,1024]{1,0:T(2,128)(2,1)S(1)}, bf16[1,1024]{1,0:T(2,128)(2,1)}, u32[]{:S(2)}) copy-start(bf16[1,1024]{1,0:T(2,128)(2,1)} %param.20) | copy-start | bytes 6148
  361.4 82.3 %collective-permute-start.11 = (bf16[1024,1024]{1,0:T(8,128)(2,1)}, bf16[1024,1024]{1,0:T(8,128)(2,1)}, u32[]{:S(2)}, u32[]{:S(2)}) collective-permute-start(bf16[1024,1024]{1,0:T(8,128)(2,1)} %get-tuple-element.34), channel_id=1, source_target_pairs={{2,0},{3,1},{0,2},{1,3},{6,4},{7,5},{4,6},{5,7},{10,8},{11,9},{8,1... | collective-permute-start | bytes 6291464 | tf_op jit(solution)/shard_map/ppermute | solution.py:35
  403.5 43.3 %collective-permute-start.10 = (bf16[896,1024]{1,0:T(8,128)(2,1)}, bf16[896,1024]{1,0:T(8,128)(2,1)}, u32[]{:S(2)}, u32[]{:S(2)}) collective-permute-start(bf16[896,1024]{1,0:T(8,128)(2,1)} %fusion.43), channel_id=1, source_target_pairs={{1,0},{0,1},{3,2},{2,3},{5,4},{4,5},{7,6},{6,7},{9,8},{8,9},{11,10... | collective-permute-start | bytes 5505032 | tf_op jit(solution)/shard_map/ppermute | solution.py:35
  407.5 89.4 %copy-start.31 = (bf16[896,1024]{1,0:T(8,128)(2,1)}, bf16[896,1024]{1,0:T(8,128)(2,1)S(1)}, u32[]{:S(2)}) copy-start(bf16[896,1024]{1,0:T(8,128)(2,1)S(1)} %fusion.26) | copy-start | bytes 5505028
  407.5 73.0 %collective-permute-start.20 = (bf16[896,1024]{1,0:T(8,128)(2,1)S(1)}, bf16[896,1024]{1,0:T(8,128)(2,1)S(1)}, u32[]{:S(2)}, u32[]{:S(2)}) collective-permute-start(bf16[896,1024]{1,0:T(8,128)(2,1)S(1)} %fusion.26), channel_id=1, source_target_pairs={{1,0},{0,1},{3,2},{2,3},{5,4},{4,5},{7,6},{6,7},{9,8},{8,9},{11,10... | collective-permute-start | bytes 5505032 | tf_op jit(solution)/shard_map/ppermute | solution.py:35
  408.2 47.8 %copy-start.24 = (bf16[1,2,1024,1024]{3,2,1,0:T(8,128)(2,1)S(1)}, bf16[1,2,1024,1024]{3,2,1,0:T(8,128)(2,1)}, u32[]{:S(2)}) copy-start(bf16[1,2,1024,1024]{3,2,1,0:T(8,128)(2,1)} %param.21) | copy-start | bytes 12582916
  408.2 88.7 %collective-permute-start.12 = (bf16[1024,1024]{1,0:T(8,128)(2,1)}, bf16[1024,1024]{1,0:T(8,128)(2,1)S(1)}, u32[]{:S(2)}, u32[]{:S(2)}) collective-permute-start(bf16[1024,1024]{1,0:T(8,128)(2,1)} %get-tuple-element.32), channel_id=1, source_target_pairs={{2,0},{3,1},{0,2},{1,3},{6,4},{7,5},{4,6},{5,7},{10,8},{11,9},{8,1... | collective-permute-start | bytes 6291464 | tf_op jit(solution)/shard_map/ppermute | solution.py:35
  516.5 76.3 %copy-start.10 = (f32[1792,1024]{1,0:T(8,128)}, f32[1792,1024]{1,0:T(8,128)S(1)}, u32[]{:S(2)}) copy-start(f32[1792,1024]{1,0:T(8,128)S(1)} %convolution_add_fusion.1) | copy-start | bytes 22020100
  516.8 43.0 %collective-permute-start.21 = (bf16[896,1024]{1,0:T(8,128)(2,1)S(1)}, bf16[896,1024]{1,0:T(8,128)(2,1)S(1)}, u32[]{:S(2)}, u32[]{:S(2)}) collective-permute-start(bf16[896,1024]{1,0:T(8,128)(2,1)S(1)} %split.73), channel_id=1, source_target_pairs={{1,0},{0,1},{3,2},{2,3},{5,4},{4,5},{7,6},{6,7},{9,8},{8,9},{11,10... | collective-permute-start | bytes 5505032 | tf_op jit(solution)/shard_map/ppermute | solution.py:35
  518.4 74.4 %slice-start.5 = ((s8[7340032]{0:T(1024)(128)(4,1)}), s8[4194304]{0:T(1024)(128)(4,1)S(1)}, s32[]{:S(2)}) async-start(s8[7340032]{0:T(1024)(128)(4,1)} %bitcast.264), calls=%async_computation.11 | async-start | bytes 8388608
  527.1 65.7 %slice-start.6 = ((s8[7340032]{0:T(1024)(128)(4,1)}), s8[3145728]{0:T(1024)(128)(4,1)S(1)}, s32[]{:S(2)}) async-start(s8[7340032]{0:T(1024)(128)(4,1)} %bitcast.264), calls=%async_computation.12 | async-start | bytes 6291456
  538.8 54.1 %collective-permute-start.13 = (bf16[896,1024]{1,0:T(8,128)(2,1)S(1)}, bf16[896,1024]{1,0:T(8,128)(2,1)}, u32[]{:S(2)}, u32[]{:S(2)}) collective-permute-start(bf16[896,1024]{1,0:T(8,128)(2,1)S(1)} %split.74), channel_id=1, source_target_pairs={{1,0},{0,1},{3,2},{2,3},{5,4},{4,5},{7,6},{6,7},{9,8},{8,9},{11,10... | collective-permute-start | bytes 5505032 | tf_op jit(solution)/shard_map/ppermute | solution.py:35
  598.9 50.4 %copy-start.28 = (bf16[896,1024]{1,0:T(8,128)(2,1)}, bf16[896,1024]{1,0:T(8,128)(2,1)S(1)}, u32[]{:S(2)}) copy-start(bf16[896,1024]{1,0:T(8,128)(2,1)S(1)} %get-tuple-element.38) | copy-start | bytes 5505028
  598.9 35.6 %collective-permute-start.22 = (bf16[896,1024]{1,0:T(8,128)(2,1)S(1)}, bf16[896,1024]{1,0:T(8,128)(2,1)S(1)}, u32[]{:S(2)}, u32[]{:S(2)}) collective-permute-start(bf16[896,1024]{1,0:T(8,128)(2,1)S(1)} %get-tuple-element.38), channel_id=1, source_target_pairs={{2,0},{3,1},{0,2},{1,3},{6,4},{7,5},{4,6},{5,7},{10,8},{11,9},{8,1... | collective-permute-start | bytes 5505032 | tf_op jit(solution)/shard_map/ppermute | solution.py:35
  670.7 35.0 %collective-permute-start.23 = (bf16[896,1024]{1,0:T(8,128)(2,1)}, bf16[896,1024]{1,0:T(8,128)(2,1)}, u32[]{:S(2)}, u32[]{:S(2)}) collective-permute-start(bf16[896,1024]{1,0:T(8,128)(2,1)} %split.72), channel_id=1, source_target_pairs={{2,0},{3,1},{0,2},{1,3},{6,4},{7,5},{4,6},{5,7},{10,8},{11,9},{8,1... | collective-permute-start | bytes 5505032 | tf_op jit(solution)/shard_map/ppermute | solution.py:35
  713.9 50.9 %all-to-all-start.1 = ((bf16[8,112,1024]{2,1,0:T(8,128)(2,1)}), bf16[8,112,1024]{2,1,0:T(8,128)(2,1)}, u32[]{:S(2)}, u32[]{:S(2)}) async-start(bf16[8,112,1024]{2,1,0:T(8,128)(2,1)} %bitcast.268), calls=%async_computation.1 | async-start | bytes 3670016 | tf_op jit(solution)/shard_map/all_to_all | solution.py:191
  730.0 48.9 %collective-permute-start.45 = (bf16[1024,1024]{1,0:T(8,128)(2,1)}, bf16[1024,1024]{1,0:T(8,128)(2,1)}, u32[]{:S(2)}, u32[]{:S(2)}) collective-permute-start(bf16[1024,1024]{1,0:T(8,128)(2,1)} %convolution_convert_fusion.1), channel_id=1, source_target_pairs={{2,0},{3,1},{0,2},{1,3},{6,4},{7,5},{4,6},{5,7},{10,8},{11,9},{8,1... | collective-permute-start | bytes 6291464 | tf_op jit(solution)/shard_map/ppermute | solution.py:35
  738.6 84.8 %collective-permute-start.43 = (bf16[1024,1024]{1,0:T(8,128)(2,1)}, bf16[1024,1024]{1,0:T(8,128)(2,1)}, u32[]{:S(2)}, u32[]{:S(2)}) collective-permute-start(bf16[1024,1024]{1,0:T(8,128)(2,1)} %convolution_convert_fusion.3), channel_id=1, source_target_pairs={{2,0},{3,1},{0,2},{1,3},{6,4},{7,5},{4,6},{5,7},{10,8},{11,9},{8,1... | collective-permute-start | bytes 6291464 | tf_op jit(solution)/shard_map/ppermute | solution.py:35
  764.8 84.2 %all-to-all-start.3 = ((bf16[8,112,1024]{2,1,0:T(8,128)(2,1)}), bf16[8,112,1024]{2,1,0:T(8,128)(2,1)}, u32[]{:S(2)}, u32[]{:S(2)}) async-start(bf16[8,112,1024]{2,1,0:T(8,128)(2,1)} %bitcast.267), calls=%async_computation.3 | async-start | bytes 3670016 | tf_op jit(solution)/shard_map/all_to_all | solution.py:191
  769.1 627.1 %all-reduce.3.cloned.1.call-start = ((), (), s32[]{:S(2)}) async-start(), calls=%async_computation.5 | async-start | bytes 8388608 | tf_op jit(solution)/shard_map/psum | solution.py:327
  769.2 54.2 %copy-start.61 = (bf16[1792,1024]{1,0:T(8,128)(2,1)S(1)}, bf16[1792,1024]{1,0:T(8,128)(2,1)}, u32[]{:S(2)}) copy-start(bf16[1792,1024]{1,0:T(8,128)(2,1)} %copy-done.60) | copy-start | bytes 11010052
  788.7 43.0 %copy-start.54 = (bf16[896,1024]{1,0:T(8,128)(2,1)S(1)}, bf16[896,1024]{1,0:T(8,128)(2,1)}, u32[]{:S(2)}) copy-start(bf16[896,1024]{1,0:T(8,128)(2,1)} %copy-done.53) | copy-start | bytes 5505028
  788.7 43.0 %copy-start.67 = (bf16[1792,1024]{1,0:T(8,128)(2,1)S(1)}, bf16[1792,1024]{1,0:T(8,128)(2,1)}, u32[]{:S(2)}) copy-start(bf16[1792,1024]{1,0:T(8,128)(2,1)} %copy-done.66) | copy-start | bytes 11010052
  839.7 26.3 %collective-permute-start.14 = (bf16[448,1024]{1,0:T(8,128)(2,1)}, bf16[448,1024]{1,0:T(8,128)(2,1)}, u32[]{:S(2)}, u32[]{:S(2)}) collective-permute-start(bf16[448,1024]{1,0:T(8,128)(2,1)} %bitcast.29), channel_id=1, source_target_pairs={{1,0},{0,1},{3,2},{2,3},{5,4},{4,5},{7,6},{6,7},{9,8},{8,9},{11,10... | collective-permute-start | bytes 2752520 | tf_op jit(solution)/shard_map/ppermute | solution.py:35
  841.3 41.7 %collective-permute-start.15 = (bf16[448,1024]{1,0:T(8,128)(2,1)}, bf16[448,1024]{1,0:T(8,128)(2,1)}, u32[]{:S(2)}, u32[]{:S(2)}) collective-permute-start(bf16[448,1024]{1,0:T(8,128)(2,1)} %bitcast.31), channel_id=1, source_target_pairs={{1,0},{0,1},{3,2},{2,3},{5,4},{4,5},{7,6},{6,7},{9,8},{8,9},{11,10... | collective-permute-start | bytes 2752520 | tf_op jit(solution)/shard_map/ppermute | solution.py:35
  847.0 39.7 %collective-permute-start.16 = (bf16[448,1024]{1,0:T(8,128)(2,1)}, bf16[448,1024]{1,0:T(8,128)(2,1)S(1)}, u32[]{:S(2)}, u32[]{:S(2)}) collective-permute-start(bf16[448,1024]{1,0:T(8,128)(2,1)} %bitcast.29), channel_id=1, source_target_pairs={{2,0},{3,1},{0,2},{1,3},{6,4},{7,5},{4,6},{5,7},{10,8},{11,9},{8,1... | collective-permute-start | bytes 2752520 | tf_op jit(solution)/shard_map/ppermute | solution.py:35
  848.4 41.8 %collective-permute-start.17 = (bf16[448,1024]{1,0:T(8,128)(2,1)}, bf16[448,1024]{1,0:T(8,128)(2,1)S(1)}, u32[]{:S(2)}, u32[]{:S(2)}) collective-permute-start(bf16[448,1024]{1,0:T(8,128)(2,1)} %bitcast.31), channel_id=1, source_target_pairs={{2,0},{3,1},{0,2},{1,3},{6,4},{7,5},{4,6},{5,7},{10,8},{11,9},{8,1... | collective-permute-start | bytes 2752520 | tf_op jit(solution)/shard_map/ppermute | solution.py:35
  850.6 51.9 %collective-permute-start.24 = (bf16[448,1024]{1,0:T(8,128)(2,1)S(1)}, bf16[448,1024]{1,0:T(8,128)(2,1)S(1)}, u32[]{:S(2)}, u32[]{:S(2)}) collective-permute-start(bf16[448,1024]{1,0:T(8,128)(2,1)S(1)} %bitcast.283), channel_id=1, source_target_pairs={{1,0},{0,1},{3,2},{2,3},{5,4},{4,5},{7,6},{6,7},{9,8},{8,9},{11,10... | collective-permute-start | bytes 2752520 | tf_op jit(solution)/shard_map/ppermute | solution.py:35
  866.0 58.5 %collective-permute-start.26 = (bf16[448,1024]{1,0:T(8,128)(2,1)S(1)}, bf16[448,1024]{1,0:T(8,128)(2,1)S(1)}, u32[]{:S(2)}, u32[]{:S(2)}) collective-permute-start(bf16[448,1024]{1,0:T(8,128)(2,1)S(1)} %bitcast.284), channel_id=1, source_target_pairs={{2,0},{3,1},{0,2},{1,3},{6,4},{7,5},{4,6},{5,7},{10,8},{11,9},{8,1... | collective-permute-start | bytes 2752520 | tf_op jit(solution)/shard_map/ppermute | solution.py:35
  883.0 39.2 %collective-permute-start.25 = (bf16[448,1024]{1,0:T(8,128)(2,1)S(1)}, bf16[448,1024]{1,0:T(8,128)(2,1)S(1)}, u32[]{:S(2)}, u32[]{:S(2)}) collective-permute-start(bf16[448,1024]{1,0:T(8,128)(2,1)S(1)} %bitcast.281), channel_id=1, source_target_pairs={{1,0},{0,1},{3,2},{2,3},{5,4},{4,5},{7,6},{6,7},{9,8},{8,9},{11,10... | collective-permute-start | bytes 2752520 | tf_op jit(solution)/shard_map/ppermute | solution.py:35
  886.7 42.8 %collective-permute-start.27 = (bf16[448,1024]{1,0:T(8,128)(2,1)S(1)}, bf16[448,1024]{1,0:T(8,128)(2,1)S(1)}, u32[]{:S(2)}, u32[]{:S(2)}) collective-permute-start(bf16[448,1024]{1,0:T(8,128)(2,1)S(1)} %bitcast.282), channel_id=1, source_target_pairs={{2,0},{3,1},{0,2},{1,3},{6,4},{7,5},{4,6},{5,7},{10,8},{11,9},{8,1... | collective-permute-start | bytes 2752520 | tf_op jit(solution)/shard_map/ppermute | solution.py:35
  890.2 327.1 %collective-permute-start.44 = (bf16[1024,1024]{1,0:T(8,128)(2,1)}, bf16[1024,1024]{1,0:T(8,128)(2,1)}, u32[]{:S(2)}, u32[]{:S(2)}) collective-permute-start(bf16[1024,1024]{1,0:T(8,128)(2,1)} %convolution_convert_fusion.2), channel_id=1, source_target_pairs={{1,0},{0,1},{3,2},{2,3},{5,4},{4,5},{7,6},{6,7},{9,8},{8,9},{11,10... | collective-permute-start | bytes 6291464 | tf_op jit(solution)/shard_map/ppermute | solution.py:35
  902.5 46.6 %collective-permute-start.18 = (bf16[448,1024]{1,0:T(8,128)(2,1)}, bf16[448,1024]{1,0:T(8,128)(2,1)S(1)}, u32[]{:S(2)}, u32[]{:S(2)}) collective-permute-start(bf16[448,1024]{1,0:T(8,128)(2,1)} %collective-permute-done.14), channel_id=1, source_target_pairs={{2,0},{3,1},{0,2},{1,3},{6,4},{7,5},{4,6},{5,7},{10,8},{11,9},{8,1... | collective-permute-start | bytes 2752520 | tf_op jit(solution)/shard_map/ppermute | solution.py:35
  922.2 44.8 %collective-permute-start.28 = (bf16[448,1024]{1,0:T(8,128)(2,1)S(1)}, bf16[448,1024]{1,0:T(8,128)(2,1)S(1)}, u32[]{:S(2)}, u32[]{:S(2)}) collective-permute-start(bf16[448,1024]{1,0:T(8,128)(2,1)S(1)} %collective-permute-done.24), channel_id=1, source_target_pairs={{2,0},{3,1},{0,2},{1,3},{6,4},{7,5},{4,6},{5,7},{10,8},{11,9},{8,1... | collective-permute-start | bytes 2752520 | tf_op jit(solution)/shard_map/ppermute | solution.py:35
  924.5 62.2 %collective-permute-start.19 = (bf16[448,1024]{1,0:T(8,128)(2,1)S(1)}, bf16[448,1024]{1,0:T(8,128)(2,1)S(1)}, u32[]{:S(2)}, u32[]{:S(2)}) collective-permute-start(bf16[448,1024]{1,0:T(8,128)(2,1)S(1)} %collective-permute-done.17), channel_id=1, source_target_pairs={{1,0},{0,1},{3,2},{2,3},{5,4},{4,5},{7,6},{6,7},{9,8},{8,9},{11,10... | collective-permute-start | bytes 2752520 | tf_op jit(solution)/shard_map/ppermute | solution.py:35
  929.5 77.0 %collective-permute-start.29 = (bf16[448,1024]{1,0:T(8,128)(2,1)S(1)}, bf16[448,1024]{1,0:T(8,128)(2,1)S(1)}, u32[]{:S(2)}, u32[]{:S(2)}) collective-permute-start(bf16[448,1024]{1,0:T(8,128)(2,1)S(1)} %collective-permute-done.27), channel_id=1, source_target_pairs={{1,0},{0,1},{3,2},{2,3},{5,4},{4,5},{7,6},{6,7},{9,8},{8,9},{11,10... | collective-permute-start | bytes 2752520 | tf_op jit(solution)/shard_map/ppermute | solution.py:35
  949.2 288.1 %collective-permute-start.42 = (bf16[1024,1024]{1,0:T(8,128)(2,1)}, bf16[1024,1024]{1,0:T(8,128)(2,1)}, u32[]{:S(2)}, u32[]{:S(2)}) collective-permute-start(bf16[1024,1024]{1,0:T(8,128)(2,1)} %convolution_convert_fusion.4), channel_id=1, source_target_pairs={{1,0},{0,1},{3,2},{2,3},{5,4},{4,5},{7,6},{6,7},{9,8},{8,9},{11,10... | collective-permute-start | bytes 6291464 | tf_op jit(solution)/shard_map/ppermute | solution.py:35
  1215.7 19.8 %collective-permute-start.31 = (bf16[768,512]{1,0:T(8,128)(2,1)S(1)}, bf16[768,512]{1,0:T(8,128)(2,1)S(1)}, u32[]{:S(2)}, u32[]{:S(2)}) collective-permute-start(bf16[768,512]{1,0:T(8,128)(2,1)S(1)} %get-tuple-element.26), channel_id=1, source_target_pairs={{1,0},{0,1},{3,2},{2,3},{5,4},{4,5},{7,6},{6,7},{9,8},{8,9},{11,10... | collective-permute-start | bytes 2359304 | tf_op jit(solution)/shard_map/ppermute | solution.py:35
  1229.4 29.9 %collective-permute-start.30 = (bf16[768,512]{1,0:T(8,128)(2,1)}, bf16[768,512]{1,0:T(8,128)(2,1)}, u32[]{:S(2)}, u32[]{:S(2)}) collective-permute-start(bf16[768,512]{1,0:T(8,128)(2,1)} %get-tuple-element.23), channel_id=1, source_target_pairs={{1,0},{0,1},{3,2},{2,3},{5,4},{4,5},{7,6},{6,7},{9,8},{8,9},{11,10... | collective-permute-start | bytes 2359304 | tf_op jit(solution)/shard_map/ppermute | solution.py:35
  1231.0 28.3 %collective-permute-start.34 = (bf16[768,512]{1,0:T(8,128)(2,1)}, bf16[768,512]{1,0:T(8,128)(2,1)}, u32[]{:S(2)}, u32[]{:S(2)}) collective-permute-start(bf16[768,512]{1,0:T(8,128)(2,1)} %get-tuple-element.24), channel_id=1, source_target_pairs={{2,0},{3,1},{0,2},{1,3},{6,4},{7,5},{4,6},{5,7},{10,8},{11,9},{8,1... | collective-permute-start | bytes 2359304 | tf_op jit(solution)/shard_map/ppermute | solution.py:35
  1235.9 32.8 %collective-permute-start.32 = (bf16[768,512]{1,0:T(8,128)(2,1)S(1)}, bf16[768,512]{1,0:T(8,128)(2,1)}, u32[]{:S(2)}, u32[]{:S(2)}) collective-permute-start(bf16[768,512]{1,0:T(8,128)(2,1)S(1)} %fusion.37), channel_id=1, source_target_pairs={{2,0},{3,1},{0,2},{1,3},{6,4},{7,5},{4,6},{5,7},{10,8},{11,9},{8,1... | collective-permute-start | bytes 2359304 | tf_op jit(solution)/shard_map/ppermute | solution.py:35
  1258.6 23.0 %collective-permute-start.33 = (bf16[768,512]{1,0:T(8,128)(2,1)S(1)}, bf16[768,512]{1,0:T(8,128)(2,1)S(1)}, u32[]{:S(2)}, u32[]{:S(2)}) collective-permute-start(bf16[768,512]{1,0:T(8,128)(2,1)S(1)} %get-tuple-element.25), channel_id=1, source_target_pairs={{2,0},{3,1},{0,2},{1,3},{6,4},{7,5},{4,6},{5,7},{10,8},{11,9},{8,1... | collective-permute-start | bytes 2359304 | tf_op jit(solution)/shard_map/ppermute | solution.py:35
  1271.4 12.1 collective-permute-start.35
  1293.1 65.9 %collective-permute-start.36 = (bf16[384,1024]{1,0:T(8,128)(2,1)}, bf16[384,1024]{1,0:T(8,128)(2,1)S(1)}, u32[]{:S(2)}, u32[]{:S(2)}) collective-permute-start(bf16[384,1024]{1,0:T(8,128)(2,1)} %get-tuple-element.42), channel_id=1, source_target_pairs={{1,0},{0,1},{3,2},{2,3},{5,4},{4,5},{7,6},{6,7},{9,8},{8,9},{11,10... | collective-permute-start | bytes 2359304 | tf_op jit(solution)/shard_map/ppermute | solution.py:35
  1293.6 67.7 %collective-permute-start.39 = (bf16[384,1024]{1,0:T(8,128)(2,1)}, bf16[384,1024]{1,0:T(8,128)(2,1)S(1)}, u32[]{:S(2)}, u32[]{:S(2)}) collective-permute-start(bf16[384,1024]{1,0:T(8,128)(2,1)} %get-tuple-element.41), channel_id=1, source_target_pairs={{2,0},{3,1},{0,2},{1,3},{6,4},{7,5},{4,6},{5,7},{10,8},{11,9},{8,1... | collective-permute-start | bytes 2359304 | tf_op jit(solution)/shard_map/ppermute | solution.py:35
  1297.9 65.0 %collective-permute-start.37 = (bf16[384,1024]{1,0:T(8,128)(2,1)}, bf16[384,1024]{1,0:T(8,128)(2,1)}, u32[]{:S(2)}, u32[]{:S(2)}) collective-permute-start(bf16[384,1024]{1,0:T(8,128)(2,1)} %get-tuple-element.41), channel_id=1, source_target_pairs={{1,0},{0,1},{3,2},{2,3},{5,4},{4,5},{7,6},{6,7},{9,8},{8,9},{11,10... | collective-permute-start | bytes 2359304 | tf_op jit(solution)/shard_map/ppermute | solution.py:35
  1299.3 65.7 %collective-permute-start.38 = (bf16[384,1024]{1,0:T(8,128)(2,1)}, bf16[384,1024]{1,0:T(8,128)(2,1)}, u32[]{:S(2)}, u32[]{:S(2)}) collective-permute-start(bf16[384,1024]{1,0:T(8,128)(2,1)} %get-tuple-element.42), channel_id=1, source_target_pairs={{2,0},{3,1},{0,2},{1,3},{6,4},{7,5},{4,6},{5,7},{10,8},{11,9},{8,1... | collective-permute-start | bytes 2359304 | tf_op jit(solution)/shard_map/ppermute | solution.py:35
  1359.0 18.9 %collective-permute-start.40 = (bf16[384,1024]{1,0:T(8,128)(2,1)S(1)}, bf16[384,1024]{1,0:T(8,128)(2,1)S(1)}, u32[]{:S(2)}, u32[]{:S(2)}) collective-permute-start(bf16[384,1024]{1,0:T(8,128)(2,1)S(1)} %collective-permute-done.36), channel_id=1, source_target_pairs={{2,0},{3,1},{0,2},{1,3},{6,4},{7,5},{4,6},{5,7},{10,8},{11,9},{8,1... | collective-permute-start | bytes 2359304 | tf_op jit(solution)/shard_map/ppermute | solution.py:35
  1361.3 17.5 %collective-permute-start.41 = (bf16[384,1024]{1,0:T(8,128)(2,1)S(1)}, bf16[384,1024]{1,0:T(8,128)(2,1)S(1)}, u32[]{:S(2)}, u32[]{:S(2)}) collective-permute-start(bf16[384,1024]{1,0:T(8,128)(2,1)S(1)} %collective-permute-done.39), channel_id=1, source_target_pairs={{1,0},{0,1},{3,2},{2,3},{5,4},{4,5},{7,6},{6,7},{9,8},{8,9},{11,10... | collective-permute-start | bytes 2359304 | tf_op jit(solution)/shard_map/ppermute | solution.py:35
  (65 other events, 835.6 us)
Sparse Core Ops, SparseCore 0:
  115.9 50.9 all-gather.1
  1298.0 98.1 all-reduce.2
where the time goes:
time: 1420 us; the launch traced here: 1410 us
  waiting for transfers between devices  494 us (35%)
  matrix products  350 us (25%)
  local copies, waits for them, and re-layouts  259 us (18%)
  other arithmetic  150 us (11%)
  starting transfers between devices  79.7 us (6%)
  blocking collectives  60.2 us (4%)
  between operations  15.8 us (1%)
    ppermute x46, waiting for transfers between devices, fetch(): return lax.ppermute(value, 'tensor', self._pairs(axis, shift))  439 us
    dot_general x27, matrix products, dot(): lax.dot_general(a, b, (contract, ((), ())), preferred_element_type=F32)  207 us
    ppermute x46, starting transfers between devices, fetch(): return lax.ppermute(value, 'tensor', self._pairs(axis, shift))  58.3 us
    psum x1, blocking collectives, body(): lax.psum(norm_parts, ('dp', 'tensor'))  49.7 us
    convert_element_type x1, other arithmetic, body(): grad_scores = (attention_weights * (grad_probs - row_delta)).astype(BF16)  42.3 us
    gather x2, local copies, waits for them, and re-layouts, from_experts(): picked = every.reshape(shards * own_rows, model_width)[tok_place]  39.8 us
    all_to_all x2, waiting for transfers between devices, to_experts(): lax.all_to_all(picked.reshape(experts, share, model_width), 'dp', split_a...  37.3 us
    dot_general x1, matrix products, body(): jnp.einsum('sqhd,skhd->shqk', grad_attended, values, preferred_element_ty...  36.9 us
  transfers between devices with their start and end apart: 52, of which 31 were waited for; matrix products, arithmetic and copies ran while one was open for 37% of the time, Pallas kernels for 0%

commit v1 on v0

--- a/solution.py
+++ b/solution.py
@@ -178,13 +178,20 @@
 
     def to_experts(rows):
         picked = jnp.where(own_filled, rows[own_index], jnp.zeros((), rows.dtype))
-        moved = lax.all_to_all(
-            picked.reshape(experts, share, model_width),
-            "dp",
-            split_axis=0,
-            concat_axis=0,
-            tiled=True,
-        )
+        value_2 = picked.reshape(experts, share, model_width)
+        ways, here = (lax.axis_size("dp"), lax.axis_index("dp"))
+        width_2 = value_2.shape[0] // ways
+        dims = list(value_2.shape)
+        dims[0] = width_2
+        height = dims[0]
+        dims[0] = height * ways
+        full = jnp.zeros(dims, value_2.dtype)
+        for mask in range(ways):
+            part = lax.dynamic_slice_in_dim(value_2, (here ^ mask) * width_2, width_2, axis=0)
+            if mask:
+                part = lax.ppermute(part, "dp", [(d, d ^ mask) for d in range(ways)])
+            full = lax.dynamic_update_slice_in_dim(full, part, (here ^ mask) * height, axis=0)
+        moved = full
         return moved.reshape(own_rows, model_width)
 
     def from_experts(rows):

time: 1420 us -> 1440 us (1.014)
  starting transfers between devices: 79.7 us -> 107 us
    ppermute x0 -> x14, waiting for transfers between devices: none -> 55.1 us  [to_experts(): part = lax.ppermute(part, 'dp', [(d, d ^ mask) for d in range(ways)])]
    all_to_all x2 -> x0, waiting for transfers between devices: 37.3 us -> none  [to_experts(): lax.all_to_all(picked.reshape(experts, share, model_width), 'dp', split_a...]
    ppermute x0 -> x14, starting transfers between devices: none -> 27.7 us  [to_experts(): part = lax.ppermute(part, 'dp', [(d, d ^ mask) for d in range(ways)])]
    ppermute x46, waiting for transfers between devices: 439 us -> 420 us  [fetch(): return lax.ppermute(value, 'tensor', self._pairs(axis, shift))]
  transfers between devices with their start and end apart: 52 -> 64, of which waited for: 31 -> 34; matrix products, arithmetic and copies ran while one was open for 37% -> 36% of each run, Pallas kernels for 0% -> 0%
where the time goes in v1:
time: 1440 us; the launch traced here: 1430 us
  waiting for transfers between devices  494 us (34%)
  matrix products  356 us (25%)
  local copies, waits for them, and re-layouts  254 us (18%)
  other arithmetic  142 us (10%)
  starting transfers between devices  107 us (7%)
  blocking collectives  60.1 us (4%)
  between operations  16 us (1%)
    ppermute x46, waiting for transfers between devices, fetch(): return lax.ppermute(value, 'tensor', self._pairs(axis, shift))  420 us
    dot_general x27, matrix products, dot(): lax.dot_general(a, b, (contract, ((), ())), preferred_element_type=F32)  213 us
    ppermute x46, starting transfers between devices, fetch(): return lax.ppermute(value, 'tensor', self._pairs(axis, shift))  56.4 us
    ppermute x14, waiting for transfers between devices, to_experts(): part = lax.ppermute(part, 'dp', [(d, d ^ mask) for d in range(ways)])  55.1 us
    psum x1, blocking collectives, body(): lax.psum(norm_parts, ('dp', 'tensor'))  49.7 us
    convert_element_type x1, other arithmetic, body(): grad_scores = (attention_weights * (grad_probs - row_delta)).astype(BF16)  42.3 us
    gather x2, local copies, waits for them, and re-layouts, from_experts(): picked = every.reshape(shards * own_rows, model_width)[tok_place]  39.8 us
    dot_general x1, matrix products, body(): jnp.einsum('sqhd,skhd->shqk', grad_attended, values, preferred_element_ty...  36.9 us
  transfers between devices with their start and end apart: 64, of which 34 were waited for; matrix products, arithmetic and copies ran while one was open for 36% of the time, Pallas kernels for 0%

profile of v1, /device:TPU:0, one launch (start us, length us, event | category | flops | bytes accessed | tf_op | source)
XLA Modules:
  0.0 1427.7 jit_solution(15949260366335496869)
XLA Ops:
  25.7 13.7 reshape.318
  46.1 19.2 %fusion = (f32[3,4,1024]{2,1,0:T(4,128)S(1)}, f32[3,4,1024,1024]{2,3,1,0:T(8,128)}) fusion(pred[3,1024,1024]{1,2,0:T(8,128)(4,1)S(1)} %broadcast_and_fusion, bf16[3,1024,4,64]{1,0,3,2:T(4,128)(2,1)S(1)} %get-tuple-element.29, bf16[3,1024,4,64]{1,0,3,2:T(4,128)(2,1)S(1)} %get-tuple-element.27), kind=kOutput, calls=%fused_computation.13 | convolution fusion | flops 1648349184 | bytes 56672256 | tf_op jit(solution)/shard_map/sqhd,skhd->shqk/dot_general | solution.py:225
  65.3 21.2 %exponential_reduce_fusion = f32[3,4,1024]{2,1,0:T(4,128)S(1)} fusion(f32[3,4,1024,1024]{2,3,1,0:T(8,128)} %get-tuple-element.70, f32[3,4,1024]{2,1,0:T(4,128)S(1)} %get-tuple-element.69, pred[3,1024,1024]{1,2,0:T(8,128)(4,1)S(1)} %broadcast_and_fusion), kind=kLoop, calls=%fused_computation.11 | loop fusion | flops 50319360 | bytes 53575680 | tf_op jit(solution)/shard_map/reduce_sum | solution.py:232
  86.5 20.1 %fusion.39 = bf16[3,1024,4,64]{1,3,2,0:T(8,128)(2,1)S(1)} fusion(bf16[3,1024,4,64]{1,0,3,2:T(4,128)(2,1)S(1)} %get-tuple-element.28, f32[3,4,1024,1024]{2,3,1,0:T(8,128)} %get-tuple-element.70, f32[3,4,1024]{2,1,0:T(4,128)S(1)} %log_add_fusion, pred[3,1024,1024]{1,2,0:T(8,128)(4,1)S(1)} %broadcast_and_fusion), kind=kOutput, calls=%fused_computation.133 | convolution fusion | flops 1661730816 | bytes 56672256 | tf_op jit(solution)/shard_map/shqk,skhd->sqhd/dot_general | solution.py:237
  122.7 19.4 %gather_fusion = pred[3072]{0:T(1024)(128)(4,1)S(1)} fusion(pred[3072]{0:T(1024)(128)(4,1)S(1)} %fusion.60, s32[3072]{0:T(1024)S(1)} %broadcast_clamp_fusion), kind=kCustom, calls=%fused_computation | custom fusion | bytes 18432 | tf_op jit(solution)/shard_map/gather | solution.py:109
  142.0 17.4 %gather_fusion.1 = s32[3072]{0:T(1024)S(1)} fusion(s32[3072]{0:T(1024)S(1)} %bitcast.249, s32[3072]{0:T(1024)S(1)} %broadcast_clamp_fusion), kind=kCustom, calls=%fused_computation.1 | custom fusion | bytes 36864 | tf_op jit(solution)/shard_map/gather | solution.py:108
  162.5 11.8 scatter_custom_fusion.1
  179.3 9.0 gather_fusion.4
  209.5 14.0 fusion.2
  223.5 9.1 gather_fusion.2
  256.3 17.1 %collective-permute-done.10 = bf16[1,112,1024]{2,1,0:T(8,128)(2,1)S(1)} collective-permute-done((bf16[1,112,1024]{2,1,0:T(8,128)(2,1)S(1)}, bf16[1,112,1024]{2,1,0:T(8,128)(2,1)S(1)}, u32[]{:S(2)}, u32[]{:S(2)}) %collective-permute-start.10) | collective-permute-done | bytes 229408 | tf_op jit(solution)/shard_map/ppermute | solution.py:192
  275.8 9.9 collective-permute-done.14
  285.7 28.5 %collective-permute-done.13 = bf16[896,1024]{1,0:T(8,128)(2,1)S(1)} collective-permute-done((bf16[896,1024]{1,0:T(8,128)(2,1)S(1)}, bf16[896,1024]{1,0:T(8,128)(2,1)S(1)}, u32[]{:S(2)}, u32[]{:S(2)}) %collective-permute-start.13) | collective-permute-done | bytes 1835040 | tf_op jit(solution)/shard_map/ppermute | solution.py:35
  314.2 8.0 multiply_convert_fusion.7
  322.2 8.6 multiply_convert_fusion.8
  330.8 8.0 fusion.85
  340.2 8.8 convolution_add_fusion.3
  351.8 40.4 %collective-permute-done.16 = bf16[896,1024]{1,0:T(8,128)(2,1)S(1)} collective-permute-done((bf16[896,1024]{1,0:T(8,128)(2,1)S(1)}, bf16[896,1024]{1,0:T(8,128)(2,1)S(1)}, u32[]{:S(2)}, u32[]{:S(2)}) %collective-permute-start.16) | collective-permute-done | bytes 1835040 | tf_op jit(solution)/shard_map/ppermute | solution.py:35
  394.0 10.5 collective-permute-start.28
  423.3 17.2 %collective-permute-done.31 = bf16[1,112,1024]{2,1,0:T(8,128)(2,1)S(1)} collective-permute-done((bf16[1,112,1024]{2,1,0:T(8,128)(2,1)S(1)}, bf16[1,112,1024]{2,1,0:T(8,128)(2,1)S(1)}, u32[]{:S(2)}, u32[]{:S(2)}) %collective-permute-start.31) | collective-permute-done | bytes 229408 | tf_op jit(solution)/shard_map/ppermute | solution.py:192
  444.4 9.6 multiply_convert_fusion.5
  454.0 8.6 multiply_convert_fusion.6
  462.6 19.6 %collective-permute-done.34 = bf16[896,1024]{1,0:T(8,128)(2,1)} collective-permute-done((bf16[896,1024]{1,0:T(8,128)(2,1)S(1)}, bf16[896,1024]{1,0:T(8,128)(2,1)}, u32[]{:S(2)}, u32[]{:S(2)}) %collective-permute-start.34) | collective-permute-done | bytes 1835040 | tf_op jit(solution)/shard_map/ppermute | solution.py:35
  482.2 10.2 multiply_convert_fusion.4
  492.4 8.1 fusion.86
  500.5 11.2 multiply_convert_fusion.3
  511.7 8.8 convolution_add_fusion.1
  531.4 11.8 convolution_add_fusion.2
  547.1 16.7 %collective-permute-done.35 = bf16[896,1024]{1,0:T(8,128)(2,1)S(1)} collective-permute-done((bf16[896,1024]{1,0:T(8,128)(2,1)S(1)}, bf16[896,1024]{1,0:T(8,128)(2,1)S(1)}, u32[]{:S(2)}, u32[]{:S(2)}) %collective-permute-start.35) | collective-permute-done | bytes 1835040 | tf_op jit(solution)/shard_map/ppermute | solution.py:35
  563.8 35.9 %collective-permute-done.20 = bf16[896,1024]{1,0:T(8,128)(2,1)} collective-permute-done((bf16[896,1024]{1,0:T(8,128)(2,1)S(1)}, bf16[896,1024]{1,0:T(8,128)(2,1)}, u32[]{:S(2)}, u32[]{:S(2)}) %collective-permute-start.20) | collective-permute-done | bytes 1835040 | tf_op jit(solution)/shard_map/ppermute | solution.py:35
  606.5 37.5 %collective-permute-done.36 = bf16[896,1024]{1,0:T(8,128)(2,1)S(1)} collective-permute-done((bf16[896,1024]{1,0:T(8,128)(2,1)}, bf16[896,1024]{1,0:T(8,128)(2,1)S(1)}, u32[]{:S(2)}, u32[]{:S(2)}) %collective-permute-start.36) | collective-permute-done | bytes 1835040 | tf_op jit(solution)/shard_map/ppermute | solution.py:35
  644.0 9.7 multiply_convert_fusion.2
  657.8 10.0 multiply_convert_fusion.1
  678.0 36.6 %collective-permute-done.37 = bf16[896,1024]{1,0:T(8,128)(2,1)} collective-permute-done((bf16[896,1024]{1,0:T(8,128)(2,1)}, bf16[896,1024]{1,0:T(8,128)(2,1)}, u32[]{:S(2)}, u32[]{:S(2)}) %collective-permute-start.37) | collective-permute-done | bytes 1835040 | tf_op jit(solution)/shard_map/ppermute | solution.py:35
  714.6 8.3 fusion.30
  723.0 18.1 %all-to-all-start = ((bf16[8,112,1024]{2,1,0:T(8,128)(2,1)}), bf16[8,112,1024]{2,1,0:T(8,128)(2,1)}, u32[]{:S(2)}, u32[]{:S(2)}) async-start(bf16[8,112,1024]{2,1,0:T(8,128)(2,1)} %bitcast.266), calls=%async_computation | async-start | bytes 3670016 | tf_op jit(solution)/shard_map/all_to_all | solution.py:198
  741.1 8.6 convolution_convert_fusion.1
  758.5 11.9 scatter_custom_fusion
  772.4 10.4 psum.31
  789.0 9.7 collective-permute-done.59
  798.7 9.8 add_bitcast_fusion
  808.5 34.7 %collective-permute-done.57 = bf16[1024,1024]{1,0:T(8,128)(2,1)} collective-permute-done((bf16[1024,1024]{1,0:T(8,128)(2,1)}, bf16[1024,1024]{1,0:T(8,128)(2,1)}, u32[]{:S(2)}, u32[]{:S(2)}) %collective-permute-start.57) | collective-permute-done | bytes 2097184 | tf_op jit(solution)/shard_map/ppermute | solution.py:35
  843.3 7.6 add_bitcast_fusion.2
  888.6 13.7 collective-permute-done.22
  911.9 10.0 collective-permute-done.38
  924.1 17.5 %collective-permute-done.39 = bf16[448,1024]{1,0:T(8,128)(2,1)S(1)} collective-permute-done((bf16[448,1024]{1,0:T(8,128)(2,1)S(1)}, bf16[448,1024]{1,0:T(8,128)(2,1)S(1)}, u32[]{:S(2)}, u32[]{:S(2)}) %collective-permute-start.39) | collective-permute-done | bytes 917536 | tf_op jit(solution)/shard_map/ppermute | solution.py:35
  952.3 16.3 %collective-permute-done.25 = bf16[448,1024]{1,0:T(8,128)(2,1)S(1)} collective-permute-done((bf16[448,1024]{1,0:T(8,128)(2,1)}, bf16[448,1024]{1,0:T(8,128)(2,1)S(1)}, u32[]{:S(2)}, u32[]{:S(2)}) %collective-permute-start.25) | collective-permute-done | bytes 917536 | tf_op jit(solution)/shard_map/ppermute | solution.py:35
  970.9 15.4 %collective-permute-done.42 = bf16[448,1024]{1,0:T(8,128)(2,1)S(1)} collective-permute-done((bf16[448,1024]{1,0:T(8,128)(2,1)S(1)}, bf16[448,1024]{1,0:T(8,128)(2,1)S(1)}, u32[]{:S(2)}, u32[]{:S(2)}) %collective-permute-start.42) | collective-permute-done | bytes 917536 | tf_op jit(solution)/shard_map/ppermute | solution.py:35
  987.3 18.8 %collective-permute-done.26 = bf16[448,1024]{1,0:T(8,128)(2,1)S(1)} collective-permute-done((bf16[448,1024]{1,0:T(8,128)(2,1)S(1)}, bf16[448,1024]{1,0:T(8,128)(2,1)S(1)}, u32[]{:S(2)}, u32[]{:S(2)}) %collective-permute-start.26) | collective-permute-done | bytes 917536 | tf_op jit(solution)/shard_map/ppermute | solution.py:35
  1006.2 19.7 %collective-permute-done.43 = bf16[448,1024]{1,0:T(8,128)(2,1)S(1)} collective-permute-done((bf16[448,1024]{1,0:T(8,128)(2,1)S(1)}, bf16[448,1024]{1,0:T(8,128)(2,1)S(1)}, u32[]{:S(2)}, u32[]{:S(2)}) %collective-permute-start.43) | collective-permute-done | bytes 917536 | tf_op jit(solution)/shard_map/ppermute | solution.py:35
  1027.2 19.9 %gather_fusion.3 = bf16[3072,1024]{1,0:T(8,128)(2,1)} fusion(bf16[3584,1024]{1,0:T(8,128)(2,1)} %bitcast.37, s32[3072]{0:T(1024)S(1)} %fusion.66), kind=kCustom, calls=%fused_computation.3 | custom fusion | bytes 12595200 | tf_op jit(solution)/shard_map/gather | solution.py:202
  1047.1 19.9 %gather_fusion.5 = bf16[3072,1024]{1,0:T(8,128)(2,1)} fusion(bf16[3584,1024]{1,0:T(8,128)(2,1)} %bitcast.51, s32[3072]{0:T(1024)S(1)} %fusion.66), kind=kCustom, calls=%fused_computation.5 | custom fusion | bytes 12595200 | tf_op jit(solution)/shard_map/gather | solution.py:202
  1067.0 17.5 %convert_add_fusion.1 = (f32[3072,1024]{1,0:T(8,128)S(1)}, bf16[3072,1024]{1,0:T(8,128)(2,1)}) fusion(bf16[3072,1024]{1,0:T(8,128)(2,1)} %param.23, bf16[3072,1024]{1,0:T(8,128)(2,1)} %gather_fusion.5, pred[3072]{0:T(1024)(128)(4,1)S(1)} %broadcast_compare_fusion, bf16[3072,1024]{1,0:T(8,128)(2,1)} %gather_fusion.3, f32[3072,1024]{1,0:T(8,128)} %get-tuple-element.72, ...), kind=kLoop, calls=%fused_computation.19 | loop fusion | flops 31457280 | bytes 56626176 | tf_op jit(solution)/shard_map/add | solution.py:288
  1098.1 36.9 %multiply_reduce_fusion = (f32[3,4,1024]{2,1,0:T(4,128)S(1)}, f32[3,4,1024,1024]{2,3,1,0:T(8,128)}) fusion(f32[3,4,1024,1024]{2,3,1,0:T(8,128)} %get-tuple-element.70, f32[3,4,1024]{2,1,0:T(4,128)S(1)} %copy-done.35, pred[3,1024,1024]{1,2,0:T(8,128)(4,1)} %copy-done.3, bf16[3,1024,4,64]{1,3,2,0:T(8,128)(2,1)S(1)} %copy.37, ...), kind=kOutput, calls=%fused_computation.9 | convolution fusion | flops 1673515008 | bytes 107053056 | tf_op jit(solution)/shard_map/sqhd,skhd->shqk/dot_general | solution.py:296
  1135.0 42.3 %multiply_convert_fusion = bf16[3,4,1024,1024]{2,3,1,0:T(8,128)(2,1)} fusion(f32[3,4,1024,1024]{2,3,1,0:T(8,128)} %get-tuple-element.82, f32[3,4,1024,1024]{2,3,1,0:T(8,128)} %get-tuple-element.70, f32[3,4,1024]{2,1,0:T(4,128)S(1)} %get-tuple-element.81, f32[3,4,1024]{2,1,0:T(4,128)S(1)} %copy-done.35, pred[3,1024,1024]{1,2,0:T(8,128)(4,1)} %copy-done.3), kind=kLoop, calls=%fused_computation.8 | loop fusion | flops 75497472 | bytes 129073152 | tf_op jit(solution)/shard_map/convert_element_type | solution.py:298
  1177.3 13.4 fusion.41
  1190.8 14.0 fusion.42
  1204.8 20.3 %fusion.40 = bf16[3,1024,4,64]{1,3,2,0:T(8,128)(2,1)S(1)} fusion(bf16[3,1024,4,64]{1,3,2,0:T(8,128)(2,1)} %copy-done.12, f32[3,4,1024,1024]{2,3,1,0:T(8,128)} %get-tuple-element.70, f32[3,4,1024]{2,1,0:T(4,128)S(1)} %copy-done.35, pred[3,1024,1024]{1,2,0:T(8,128)(4,1)} %copy-done.3), kind=kOutput, calls=%fused_computation.134 | convolution fusion | flops 1661730816 | bytes 56672256 | tf_op jit(solution)/shard_map/shqk,sqhd->skhd/dot_general | solution.py:307
  1256.6 9.3 add_bitcast_fusion.3
  1278.8 9.1 collective-permute-done.46
  1319.4 8.5 maximum_bitcast_fusion
  1328.0 49.7 %psum.28 = f32[2,1024]{1,0:T(2,128)S(1)} all-reduce(f32[2,1024]{1,0:T(2,128)S(1)} %pad_maximum_fusion.6), channel_id=1, replica_groups=mesh['dp'=8,'tensor'=4] {'dp','tensor'}, use_global_device_ids=true, to_apply=%region_15.16 | all-reduce | flops 2048 | bytes 16384 | tf_op jit(solution)/shard_map/psum | solution.py:329
  1387.4 9.8 collective-permute-done.54
  1399.0 16.4 %all-reduce.3.cloned.1.call-done = (f32[1024,4,192]{0,2,1:T(8,128)}, f32[4,64,1024]{2,1,0:T(8,128)}) async-done(((f32[1024,4,192]{0,2,1:T(8,128)}, f32[4,64,1024]{2,1,0:T(8,128)}), (f32[1024,4,192]{0,2,1:T(8,128)}, f32[4,64,1024]{2,1,0:T(8,128)})) %all-reduce.3.cloned.1.call-update) | async-done | bytes 4194320 | tf_op jit(solution)/shard_map/psum | solution.py:334
  (389 shorter events, 347.9 us)
Async XLA Ops:
  7.2 202.3 %all-gather.2.cloned.1.call-start = ((), (), s32[]{:S(2)}) async-start(), calls=%async_computation.2 | async-start | bytes 2621440 | tf_op jit(solution)/shard_map/all_gather | solution.py:165
  112.5 76.0 %collective-permute-start = (bf16[1536,256]{0,1:T(8,128)(2,1)}, bf16[1536,256]{0,1:T(8,128)(2,1)}, u32[]{:S(2)}, u32[]{:S(2)}) collective-permute-start(bf16[1536,256]{0,1:T(8,128)(2,1)} %get-tuple-element.60), channel_id=1, source_target_pairs={{1,0},{0,1},{3,2},{2,3},{5,4},{4,5},{7,6},{6,7},{9,8},{8,9},{11,10... | collective-permute-start | bytes 2359304 | tf_op jit(solution)/shard_map/ppermute | solution.py:35
  115.4 80.7 %collective-permute-start.2 = (bf16[1536,256]{0,1:T(8,128)(2,1)}, bf16[1536,256]{0,1:T(8,128)(2,1)}, u32[]{:S(2)}, u32[]{:S(2)}) collective-permute-start(bf16[1536,256]{0,1:T(8,128)(2,1)} %get-tuple-element.60), channel_id=1, source_target_pairs={{2,0},{3,1},{0,2},{1,3},{6,4},{7,5},{4,6},{5,7},{10,8},{11,9},{8,1... | collective-permute-start | bytes 2359304 | tf_op jit(solution)/shard_map/ppermute | solution.py:35
  116.9 77.1 %collective-permute-start.1 = (bf16[1536,256]{0,1:T(8,128)(2,1)}, bf16[1536,256]{0,1:T(8,128)(2,1)}, u32[]{:S(2)}, u32[]{:S(2)}) collective-permute-start(bf16[1536,256]{0,1:T(8,128)(2,1)} %get-tuple-element.59), channel_id=1, source_target_pairs={{1,0},{0,1},{3,2},{2,3},{5,4},{4,5},{7,6},{6,7},{9,8},{8,9},{11,10... | collective-permute-start | bytes 2359304 | tf_op jit(solution)/shard_map/ppermute | solution.py:35
  117.5 73.0 %collective-permute-start.3 = (bf16[1536,256]{0,1:T(8,128)(2,1)}, bf16[1536,256]{0,1:T(8,128)(2,1)}, u32[]{:S(2)}, u32[]{:S(2)}) collective-permute-start(bf16[1536,256]{0,1:T(8,128)(2,1)} %get-tuple-element.59), channel_id=1, source_target_pairs={{2,0},{3,1},{0,2},{1,3},{6,4},{7,5},{4,6},{5,7},{10,8},{11,9},{8,1... | collective-permute-start | bytes 2359304 | tf_op jit(solution)/shard_map/ppermute | solution.py:35
  188.5 18.7 %collective-permute-start.4 = (bf16[1536,256]{0,1:T(8,128)(2,1)}, bf16[1536,256]{0,1:T(8,128)(2,1)S(1)}, u32[]{:S(2)}, u32[]{:S(2)}) collective-permute-start(bf16[1536,256]{0,1:T(8,128)(2,1)} %collective-permute-done), channel_id=1, source_target_pairs={{2,0},{3,1},{0,2},{1,3},{6,4},{7,5},{4,6},{5,7},{10,8},{11,9},{8,1... | collective-permute-start | bytes 2359304 | tf_op jit(solution)/shard_map/ppermute | solution.py:35
  190.5 18.1 %collective-permute-start.5 = (bf16[1536,256]{0,1:T(8,128)(2,1)}, bf16[1536,256]{0,1:T(8,128)(2,1)S(1)}, u32[]{:S(2)}, u32[]{:S(2)}) collective-permute-start(bf16[1536,256]{0,1:T(8,128)(2,1)} %collective-permute-done.3), channel_id=1, source_target_pairs={{1,0},{0,1},{3,2},{2,3},{5,4},{4,5},{7,6},{6,7},{9,8},{8,9},{11,10... | collective-permute-start | bytes 2359304 | tf_op jit(solution)/shard_map/ppermute | solution.py:35
  234.9 6.4 collective-permute-start.6
  235.0 15.0 %collective-permute-start.7 = (bf16[1,112,1024]{2,1,0:T(8,128)(2,1)S(1)}, bf16[1,112,1024]{2,1,0:T(8,128)(2,1)S(1)}, u32[]{:S(2)}, u32[]{:S(2)}) collective-permute-start(bf16[1,112,1024]{2,1,0:T(8,128)(2,1)S(1)} %get-tuple-element.46), channel_id=1, source_target_pairs={{0,8},{4,12},{8,0},{12,4},{16,24},{20,28},{24,16},{28,20},{1,9},{5... | collective-permute-start | bytes 688136 | tf_op jit(solution)/shard_map/ppermute | solution.py:192
  237.1 48.5 %collective-permute-start.14 = (bf16[1024,1024]{1,0:T(8,128)(2,1)S(1)}, bf16[1024,1024]{1,0:T(8,128)(2,1)S(1)}, u32[]{:S(2)}, u32[]{:S(2)}) collective-permute-start(bf16[1024,1024]{1,0:T(8,128)(2,1)S(1)} %get-tuple-element.35), channel_id=1, source_target_pairs={{1,0},{0,1},{3,2},{2,3},{5,4},{4,5},{7,6},{6,7},{9,8},{8,9},{11,10... | collective-permute-start | bytes 6291464 | tf_op jit(solution)/shard_map/ppermute | solution.py:35
  238.7 15.6 %collective-permute-start.8 = (bf16[1,112,1024]{2,1,0:T(8,128)(2,1)S(1)}, bf16[1,112,1024]{2,1,0:T(8,128)(2,1)S(1)}, u32[]{:S(2)}, u32[]{:S(2)}) collective-permute-start(bf16[1,112,1024]{2,1,0:T(8,128)(2,1)S(1)} %get-tuple-element.45), channel_id=1, source_target_pairs={{0,12},{4,8},{8,4},{12,0},{16,28},{20,24},{24,20},{28,16},{1,13},{... | collective-permute-start | bytes 688136 | tf_op jit(solution)/shard_map/ppermute | solution.py:192
  238.7 17.6 %collective-permute-start.9 = (bf16[1,112,1024]{2,1,0:T(8,128)(2,1)S(1)}, bf16[1,112,1024]{2,1,0:T(8,128)(2,1)S(1)}, u32[]{:S(2)}, u32[]{:S(2)}) collective-permute-start(bf16[1,112,1024]{2,1,0:T(8,128)(2,1)S(1)} %get-tuple-element.44), channel_id=1, source_target_pairs={{0,16},{4,20},{8,24},{12,28},{16,0},{20,4},{24,8},{28,12},{1,17},{... | collective-permute-start | bytes 688136 | tf_op jit(solution)/shard_map/ppermute | solution.py:192
  241.3 32.1 %collective-permute-start.10 = (bf16[1,112,1024]{2,1,0:T(8,128)(2,1)S(1)}, bf16[1,112,1024]{2,1,0:T(8,128)(2,1)S(1)}, u32[]{:S(2)}, u32[]{:S(2)}) collective-permute-start(bf16[1,112,1024]{2,1,0:T(8,128)(2,1)S(1)} %get-tuple-element.43), channel_id=1, source_target_pairs={{0,20},{4,16},{8,28},{12,24},{16,4},{20,0},{24,12},{28,8},{1,21},{... | collective-permute-start | bytes 688136 | tf_op jit(solution)/shard_map/ppermute | solution.py:192
  250.0 23.4 %collective-permute-start.11 = (bf16[1,112,1024]{2,1,0:T(8,128)(2,1)S(1)}, bf16[1,112,1024]{2,1,0:T(8,128)(2,1)S(1)}, u32[]{:S(2)}, u32[]{:S(2)}) collective-permute-start(bf16[1,112,1024]{2,1,0:T(8,128)(2,1)S(1)} %get-tuple-element.42), channel_id=1, source_target_pairs={{0,24},{4,28},{8,16},{12,20},{16,8},{20,12},{24,0},{28,4},{1,25},{... | collective-permute-start | bytes 688136 | tf_op jit(solution)/shard_map/ppermute | solution.py:192
  254.3 19.1 %collective-permute-start.12 = (bf16[1,112,1024]{2,1,0:T(8,128)(2,1)S(1)}, bf16[1,112,1024]{2,1,0:T(8,128)(2,1)S(1)}, u32[]{:S(2)}, u32[]{:S(2)}) collective-permute-start(bf16[1,112,1024]{2,1,0:T(8,128)(2,1)S(1)} %get-tuple-element.41), channel_id=1, source_target_pairs={{0,28},{4,24},{8,20},{12,16},{16,12},{20,8},{24,4},{28,0},{1,29},{... | collective-permute-start | bytes 688136 | tf_op jit(solution)/shard_map/ppermute | solution.py:192
  273.5 40.7 %collective-permute-start.13 = (bf16[896,1024]{1,0:T(8,128)(2,1)S(1)}, bf16[896,1024]{1,0:T(8,128)(2,1)S(1)}, u32[]{:S(2)}, u32[]{:S(2)}) collective-permute-start(bf16[896,1024]{1,0:T(8,128)(2,1)S(1)} %bitcast.254), channel_id=1, source_target_pairs={{2,0},{3,1},{0,2},{1,3},{6,4},{7,5},{4,6},{5,7},{10,8},{11,9},{8,1... | collective-permute-start | bytes 5505032 | tf_op jit(solution)/shard_map/ppermute | solution.py:35
  275.2 63.6 %collective-permute-start.15 = (bf16[1024,1024]{1,0:T(8,128)(2,1)S(1)}, bf16[1024,1024]{1,0:T(8,128)(2,1)S(1)}, u32[]{:S(2)}, u32[]{:S(2)}) collective-permute-start(bf16[1024,1024]{1,0:T(8,128)(2,1)S(1)} %get-tuple-element.33), channel_id=1, source_target_pairs={{1,0},{0,1},{3,2},{2,3},{5,4},{4,5},{7,6},{6,7},{9,8},{8,9},{11,10... | collective-permute-start | bytes 6291464 | tf_op jit(solution)/shard_map/ppermute | solution.py:35
  349.2 43.0 %collective-permute-start.16 = (bf16[896,1024]{1,0:T(8,128)(2,1)S(1)}, bf16[896,1024]{1,0:T(8,128)(2,1)S(1)}, u32[]{:S(2)}, u32[]{:S(2)}) collective-permute-start(bf16[896,1024]{1,0:T(8,128)(2,1)S(1)} %split.75), channel_id=1, source_target_pairs={{2,0},{3,1},{0,2},{1,3},{6,4},{7,5},{4,6},{5,7},{10,8},{11,9},{8,1... | collective-permute-start | bytes 5505032 | tf_op jit(solution)/shard_map/ppermute | solution.py:35
  350.5 93.9 %collective-permute-start.18 = (bf16[1024,1024]{1,0:T(8,128)(2,1)S(1)}, bf16[1024,1024]{1,0:T(8,128)(2,1)}, u32[]{:S(2)}, u32[]{:S(2)}) collective-permute-start(bf16[1024,1024]{1,0:T(8,128)(2,1)S(1)} %get-tuple-element.34), channel_id=1, source_target_pairs={{2,0},{3,1},{0,2},{1,3},{6,4},{7,5},{4,6},{5,7},{10,8},{11,9},{8,1... | collective-permute-start | bytes 6291464 | tf_op jit(solution)/shard_map/ppermute | solution.py:35
  351.7 52.7 %collective-permute-start.27 = (bf16[1,112,1024]{2,1,0:T(8,128)(2,1)S(1)}, bf16[1,112,1024]{2,1,0:T(8,128)(2,1)S(1)}, u32[]{:S(2)}, u32[]{:S(2)}) collective-permute-start(bf16[1,112,1024]{2,1,0:T(8,128)(2,1)S(1)} %get-tuple-element.55), channel_id=1, source_target_pairs={{0,4},{4,0},{8,12},{12,8},{16,20},{20,16},{24,28},{28,24},{1,5},{5... | collective-permute-start | bytes 688136 | tf_op jit(solution)/shard_map/ppermute | solution.py:192
  393.4 51.1 %collective-permute-start.17 = (bf16[896,1024]{1,0:T(8,128)(2,1)S(1)}, bf16[896,1024]{1,0:T(8,128)(2,1)}, u32[]{:S(2)}, u32[]{:S(2)}) collective-permute-start(bf16[896,1024]{1,0:T(8,128)(2,1)S(1)} %fusion.43), channel_id=1, source_target_pairs={{1,0},{0,1},{3,2},{2,3},{5,4},{4,5},{7,6},{6,7},{9,8},{8,9},{11,10... | collective-permute-start | bytes 5505032 | tf_op jit(solution)/shard_map/ppermute | solution.py:35
  394.0 20.3 %collective-permute-start.28 = (bf16[1,112,1024]{2,1,0:T(8,128)(2,1)S(1)}, bf16[1,112,1024]{2,1,0:T(8,128)(2,1)S(1)}, u32[]{:S(2)}, u32[]{:S(2)}) collective-permute-start(bf16[1,112,1024]{2,1,0:T(8,128)(2,1)S(1)} %get-tuple-element.54), channel_id=1, source_target_pairs={{0,8},{4,12},{8,0},{12,4},{16,24},{20,28},{24,16},{28,20},{1,9},{5... | collective-permute-start | bytes 688136 | tf_op jit(solution)/shard_map/ppermute | solution.py:192
  404.4 13.6 collective-permute-start.29
  404.4 16.6 %collective-permute-start.30 = (bf16[1,112,1024]{2,1,0:T(8,128)(2,1)S(1)}, bf16[1,112,1024]{2,1,0:T(8,128)(2,1)S(1)}, u32[]{:S(2)}, u32[]{:S(2)}) collective-permute-start(bf16[1,112,1024]{2,1,0:T(8,128)(2,1)S(1)} %get-tuple-element.52), channel_id=1, source_target_pairs={{0,16},{4,20},{8,24},{12,28},{16,0},{20,4},{24,8},{28,12},{1,17},{... | collective-permute-start | bytes 688136 | tf_op jit(solution)/shard_map/ppermute | solution.py:192
  414.3 26.2 %collective-permute-start.31 = (bf16[1,112,1024]{2,1,0:T(8,128)(2,1)S(1)}, bf16[1,112,1024]{2,1,0:T(8,128)(2,1)S(1)}, u32[]{:S(2)}, u32[]{:S(2)}) collective-permute-start(bf16[1,112,1024]{2,1,0:T(8,128)(2,1)S(1)} %get-tuple-element.51), channel_id=1, source_target_pairs={{0,20},{4,16},{8,28},{12,24},{16,4},{20,0},{24,12},{28,8},{1,21},{... | collective-permute-start | bytes 688136 | tf_op jit(solution)/shard_map/ppermute | solution.py:192
  418.0 22.5 %collective-permute-start.32 = (bf16[1,112,1024]{2,1,0:T(8,128)(2,1)S(1)}, bf16[1,112,1024]{2,1,0:T(8,128)(2,1)S(1)}, u32[]{:S(2)}, u32[]{:S(2)}) collective-permute-start(bf16[1,112,1024]{2,1,0:T(8,128)(2,1)S(1)} %get-tuple-element.50), channel_id=1, source_target_pairs={{0,24},{4,28},{8,16},{12,20},{16,8},{20,12},{24,0},{28,4},{1,25},{... | collective-permute-start | bytes 688136 | tf_op jit(solution)/shard_map/ppermute | solution.py:192
  421.0 19.5 %collective-permute-start.33 = (bf16[1,112,1024]{2,1,0:T(8,128)(2,1)S(1)}, bf16[1,112,1024]{2,1,0:T(8,128)(2,1)S(1)}, u32[]{:S(2)}, u32[]{:S(2)}) collective-permute-start(bf16[1,112,1024]{2,1,0:T(8,128)(2,1)S(1)} %get-tuple-element.49), channel_id=1, source_target_pairs={{0,28},{4,24},{8,20},{12,16},{16,12},{20,8},{24,4},{28,0},{1,29},{... | collective-permute-start | bytes 688136 | tf_op jit(solution)/shard_map/ppermute | solution.py:192
  441.7 40.5 %collective-permute-start.34 = (bf16[896,1024]{1,0:T(8,128)(2,1)S(1)}, bf16[896,1024]{1,0:T(8,128)(2,1)}, u32[]{:S(2)}, u32[]{:S(2)}) collective-permute-start(bf16[896,1024]{1,0:T(8,128)(2,1)S(1)} %fusion.26), channel_id=1, source_target_pairs={{1,0},{0,1},{3,2},{2,3},{5,4},{4,5},{7,6},{6,7},{9,8},{8,9},{11,10... | collective-permute-start | bytes 5505032 | tf_op jit(solution)/shard_map/ppermute | solution.py:35
  443.2 57.2 %collective-permute-start.19 = (bf16[1024,1024]{1,0:T(8,128)(2,1)S(1)}, bf16[1024,1024]{1,0:T(8,128)(2,1)}, u32[]{:S(2)}, u32[]{:S(2)}) collective-permute-start(bf16[1024,1024]{1,0:T(8,128)(2,1)S(1)} %get-tuple-element.32), channel_id=1, source_target_pairs={{2,0},{3,1},{0,2},{1,3},{6,4},{7,5},{4,6},{5,7},{10,8},{11,9},{8,1... | collective-permute-start | bytes 6291464 | tf_op jit(solution)/shard_map/ppermute | solution.py:35
  520.8 43.0 %collective-permute-start.35 = (bf16[896,1024]{1,0:T(8,128)(2,1)S(1)}, bf16[896,1024]{1,0:T(8,128)(2,1)S(1)}, u32[]{:S(2)}, u32[]{:S(2)}) collective-permute-start(bf16[896,1024]{1,0:T(8,128)(2,1)S(1)} %split.73), channel_id=1, source_target_pairs={{1,0},{0,1},{3,2},{2,3},{5,4},{4,5},{7,6},{6,7},{9,8},{8,9},{11,10... | collective-permute-start | bytes 5505032 | tf_op jit(solution)/shard_map/ppermute | solution.py:35
  545.5 54.2 %collective-permute-start.20 = (bf16[896,1024]{1,0:T(8,128)(2,1)S(1)}, bf16[896,1024]{1,0:T(8,128)(2,1)}, u32[]{:S(2)}, u32[]{:S(2)}) collective-permute-start(bf16[896,1024]{1,0:T(8,128)(2,1)S(1)} %split.74), channel_id=1, source_target_pairs={{1,0},{0,1},{3,2},{2,3},{5,4},{4,5},{7,6},{6,7},{9,8},{8,9},{11,10... | collective-permute-start | bytes 5505032 | tf_op jit(solution)/shard_map/ppermute | solution.py:35
  605.3 38.7 %collective-permute-start.36 = (bf16[896,1024]{1,0:T(8,128)(2,1)}, bf16[896,1024]{1,0:T(8,128)(2,1)S(1)}, u32[]{:S(2)}, u32[]{:S(2)}) collective-permute-start(bf16[896,1024]{1,0:T(8,128)(2,1)} %get-tuple-element.38), channel_id=1, source_target_pairs={{2,0},{3,1},{0,2},{1,3},{6,4},{7,5},{4,6},{5,7},{10,8},{11,9},{8,1... | collective-permute-start | bytes 5505032 | tf_op jit(solution)/shard_map/ppermute | solution.py:35
  676.8 37.9 %collective-permute-start.37 = (bf16[896,1024]{1,0:T(8,128)(2,1)}, bf16[896,1024]{1,0:T(8,128)(2,1)}, u32[]{:S(2)}, u32[]{:S(2)}) collective-permute-start(bf16[896,1024]{1,0:T(8,128)(2,1)} %split.72), channel_id=1, source_target_pairs={{2,0},{3,1},{0,2},{1,3},{6,4},{7,5},{4,6},{5,7},{10,8},{11,9},{8,1... | collective-permute-start | bytes 5505032 | tf_op jit(solution)/shard_map/ppermute | solution.py:35
  723.0 61.6 %all-to-all-start = ((bf16[8,112,1024]{2,1,0:T(8,128)(2,1)}), bf16[8,112,1024]{2,1,0:T(8,128)(2,1)}, u32[]{:S(2)}, u32[]{:S(2)}) async-start(bf16[8,112,1024]{2,1,0:T(8,128)(2,1)} %bitcast.266), calls=%async_computation | async-start | bytes 3670016 | tf_op jit(solution)/shard_map/all_to_all | solution.py:198
  749.8 48.9 %collective-permute-start.59 = (bf16[1024,1024]{1,0:T(8,128)(2,1)}, bf16[1024,1024]{1,0:T(8,128)(2,1)}, u32[]{:S(2)}, u32[]{:S(2)}) collective-permute-start(bf16[1024,1024]{1,0:T(8,128)(2,1)} %convolution_convert_fusion.1), channel_id=1, source_target_pairs={{2,0},{3,1},{0,2},{1,3},{6,4},{7,5},{4,6},{5,7},{10,8},{11,9},{8,1... | collective-permute-start | bytes 6291464 | tf_op jit(solution)/shard_map/ppermute | solution.py:35
  757.7 85.5 %collective-permute-start.57 = (bf16[1024,1024]{1,0:T(8,128)(2,1)}, bf16[1024,1024]{1,0:T(8,128)(2,1)}, u32[]{:S(2)}, u32[]{:S(2)}) collective-permute-start(bf16[1024,1024]{1,0:T(8,128)(2,1)} %convolution_convert_fusion.3), channel_id=1, source_target_pairs={{2,0},{3,1},{0,2},{1,3},{6,4},{7,5},{4,6},{5,7},{10,8},{11,9},{8,1... | collective-permute-start | bytes 6291464 | tf_op jit(solution)/shard_map/ppermute | solution.py:35
  784.6 83.8 %all-to-all-start.1 = ((bf16[8,112,1024]{2,1,0:T(8,128)(2,1)}), bf16[8,112,1024]{2,1,0:T(8,128)(2,1)}, u32[]{:S(2)}, u32[]{:S(2)}) async-start(bf16[8,112,1024]{2,1,0:T(8,128)(2,1)} %bitcast.265), calls=%async_computation.1 | async-start | bytes 3670016 | tf_op jit(solution)/shard_map/all_to_all | solution.py:198
  788.9 626.5 %all-reduce.3.cloned.1.call-start = ((), (), s32[]{:S(2)}) async-start(), calls=%async_computation.3 | async-start | bytes 8388608 | tf_op jit(solution)/shard_map/psum | solution.py:334
  859.1 26.1 %collective-permute-start.21 = (bf16[448,1024]{1,0:T(8,128)(2,1)}, bf16[448,1024]{1,0:T(8,128)(2,1)}, u32[]{:S(2)}, u32[]{:S(2)}) collective-permute-start(bf16[448,1024]{1,0:T(8,128)(2,1)} %bitcast.29), channel_id=1, source_target_pairs={{1,0},{0,1},{3,2},{2,3},{5,4},{4,5},{7,6},{6,7},{9,8},{8,9},{11,10... | collective-permute-start | bytes 2752520 | tf_op jit(solution)/shard_map/ppermute | solution.py:35
  860.5 41.9 %collective-permute-start.22 = (bf16[448,1024]{1,0:T(8,128)(2,1)}, bf16[448,1024]{1,0:T(8,128)(2,1)}, u32[]{:S(2)}, u32[]{:S(2)}) collective-permute-start(bf16[448,1024]{1,0:T(8,128)(2,1)} %bitcast.31), channel_id=1, source_target_pairs={{1,0},{0,1},{3,2},{2,3},{5,4},{4,5},{7,6},{6,7},{9,8},{8,9},{11,10... | collective-permute-start | bytes 2752520 | tf_op jit(solution)/shard_map/ppermute | solution.py:35
  866.4 39.5 %collective-permute-start.23 = (bf16[448,1024]{1,0:T(8,128)(2,1)}, bf16[448,1024]{1,0:T(8,128)(2,1)S(1)}, u32[]{:S(2)}, u32[]{:S(2)}) collective-permute-start(bf16[448,1024]{1,0:T(8,128)(2,1)} %bitcast.29), channel_id=1, source_target_pairs={{2,0},{3,1},{0,2},{1,3},{6,4},{7,5},{4,6},{5,7},{10,8},{11,9},{8,1... | collective-permute-start | bytes 2752520 | tf_op jit(solution)/shard_map/ppermute | solution.py:35
  867.6 41.9 %collective-permute-start.24 = (bf16[448,1024]{1,0:T(8,128)(2,1)}, bf16[448,1024]{1,0:T(8,128)(2,1)S(1)}, u32[]{:S(2)}, u32[]{:S(2)}) collective-permute-start(bf16[448,1024]{1,0:T(8,128)(2,1)} %bitcast.31), channel_id=1, source_target_pairs={{2,0},{3,1},{0,2},{1,3},{6,4},{7,5},{4,6},{5,7},{10,8},{11,9},{8,1... | collective-permute-start | bytes 2752520 | tf_op jit(solution)/shard_map/ppermute | solution.py:35
  870.1 51.9 %collective-permute-start.38 = (bf16[448,1024]{1,0:T(8,128)(2,1)S(1)}, bf16[448,1024]{1,0:T(8,128)(2,1)S(1)}, u32[]{:S(2)}, u32[]{:S(2)}) collective-permute-start(bf16[448,1024]{1,0:T(8,128)(2,1)S(1)} %bitcast.281), channel_id=1, source_target_pairs={{1,0},{0,1},{3,2},{2,3},{5,4},{4,5},{7,6},{6,7},{9,8},{8,9},{11,10... | collective-permute-start | bytes 2752520 | tf_op jit(solution)/shard_map/ppermute | solution.py:35
  885.2 58.6 %collective-permute-start.40 = (bf16[448,1024]{1,0:T(8,128)(2,1)S(1)}, bf16[448,1024]{1,0:T(8,128)(2,1)S(1)}, u32[]{:S(2)}, u32[]{:S(2)}) collective-permute-start(bf16[448,1024]{1,0:T(8,128)(2,1)S(1)} %bitcast.282), channel_id=1, source_target_pairs={{2,0},{3,1},{0,2},{1,3},{6,4},{7,5},{4,6},{5,7},{10,8},{11,9},{8,1... | collective-permute-start | bytes 2752520 | tf_op jit(solution)/shard_map/ppermute | solution.py:35
  902.4 39.2 %collective-permute-start.39 = (bf16[448,1024]{1,0:T(8,128)(2,1)S(1)}, bf16[448,1024]{1,0:T(8,128)(2,1)S(1)}, u32[]{:S(2)}, u32[]{:S(2)}) collective-permute-start(bf16[448,1024]{1,0:T(8,128)(2,1)S(1)} %bitcast.279), channel_id=1, source_target_pairs={{1,0},{0,1},{3,2},{2,3},{5,4},{4,5},{7,6},{6,7},{9,8},{8,9},{11,10... | collective-permute-start | bytes 2752520 | tf_op jit(solution)/shard_map/ppermute | solution.py:35
  905.9 43.0 %collective-permute-start.41 = (bf16[448,1024]{1,0:T(8,128)(2,1)S(1)}, bf16[448,1024]{1,0:T(8,128)(2,1)S(1)}, u32[]{:S(2)}, u32[]{:S(2)}) collective-permute-start(bf16[448,1024]{1,0:T(8,128)(2,1)S(1)} %bitcast.280), channel_id=1, source_target_pairs={{2,0},{3,1},{0,2},{1,3},{6,4},{7,5},{4,6},{5,7},{10,8},{11,9},{8,1... | collective-permute-start | bytes 2752520 | tf_op jit(solution)/shard_map/ppermute | solution.py:35
  909.6 326.9 %collective-permute-start.58 = (bf16[1024,1024]{1,0:T(8,128)(2,1)}, bf16[1024,1024]{1,0:T(8,128)(2,1)}, u32[]{:S(2)}, u32[]{:S(2)}) collective-permute-start(bf16[1024,1024]{1,0:T(8,128)(2,1)} %convolution_convert_fusion.2), channel_id=1, source_target_pairs={{1,0},{0,1},{3,2},{2,3},{5,4},{4,5},{7,6},{6,7},{9,8},{8,9},{11,10... | collective-permute-start | bytes 6291464 | tf_op jit(solution)/shard_map/ppermute | solution.py:35
  921.9 46.7 %collective-permute-start.25 = (bf16[448,1024]{1,0:T(8,128)(2,1)}, bf16[448,1024]{1,0:T(8,128)(2,1)S(1)}, u32[]{:S(2)}, u32[]{:S(2)}) collective-permute-start(bf16[448,1024]{1,0:T(8,128)(2,1)} %collective-permute-done.21), channel_id=1, source_target_pairs={{2,0},{3,1},{0,2},{1,3},{6,4},{7,5},{4,6},{5,7},{10,8},{11,9},{8,1... | collective-permute-start | bytes 2752520 | tf_op jit(solution)/shard_map/ppermute | solution.py:35
  941.6 44.8 %collective-permute-start.42 = (bf16[448,1024]{1,0:T(8,128)(2,1)S(1)}, bf16[448,1024]{1,0:T(8,128)(2,1)S(1)}, u32[]{:S(2)}, u32[]{:S(2)}) collective-permute-start(bf16[448,1024]{1,0:T(8,128)(2,1)S(1)} %collective-permute-done.38), channel_id=1, source_target_pairs={{2,0},{3,1},{0,2},{1,3},{6,4},{7,5},{4,6},{5,7},{10,8},{11,9},{8,1... | collective-permute-start | bytes 2752520 | tf_op jit(solution)/shard_map/ppermute | solution.py:35
  943.8 62.4 %collective-permute-start.26 = (bf16[448,1024]{1,0:T(8,128)(2,1)S(1)}, bf16[448,1024]{1,0:T(8,128)(2,1)S(1)}, u32[]{:S(2)}, u32[]{:S(2)}) collective-permute-start(bf16[448,1024]{1,0:T(8,128)(2,1)S(1)} %collective-permute-done.24), channel_id=1, source_target_pairs={{1,0},{0,1},{3,2},{2,3},{5,4},{4,5},{7,6},{6,7},{9,8},{8,9},{11,10... | collective-permute-start | bytes 2752520 | tf_op jit(solution)/shard_map/ppermute | solution.py:35
  948.9 76.9 %collective-permute-start.43 = (bf16[448,1024]{1,0:T(8,128)(2,1)S(1)}, bf16[448,1024]{1,0:T(8,128)(2,1)S(1)}, u32[]{:S(2)}, u32[]{:S(2)}) collective-permute-start(bf16[448,1024]{1,0:T(8,128)(2,1)S(1)} %collective-permute-done.41), channel_id=1, source_target_pairs={{1,0},{0,1},{3,2},{2,3},{5,4},{4,5},{7,6},{6,7},{9,8},{8,9},{11,10... | collective-permute-start | bytes 2752520 | tf_op jit(solution)/shard_map/ppermute | solution.py:35
  968.6 288.0 %collective-permute-start.56 = (bf16[1024,1024]{1,0:T(8,128)(2,1)}, bf16[1024,1024]{1,0:T(8,128)(2,1)}, u32[]{:S(2)}, u32[]{:S(2)}) collective-permute-start(bf16[1024,1024]{1,0:T(8,128)(2,1)} %convolution_convert_fusion.4), channel_id=1, source_target_pairs={{1,0},{0,1},{3,2},{2,3},{5,4},{4,5},{7,6},{6,7},{9,8},{8,9},{11,10... | collective-permute-start | bytes 6291464 | tf_op jit(solution)/shard_map/ppermute | solution.py:35
  1235.1 19.9 %collective-permute-start.45 = (bf16[768,512]{1,0:T(8,128)(2,1)S(1)}, bf16[768,512]{1,0:T(8,128)(2,1)S(1)}, u32[]{:S(2)}, u32[]{:S(2)}) collective-permute-start(bf16[768,512]{1,0:T(8,128)(2,1)S(1)} %get-tuple-element.26), channel_id=1, source_target_pairs={{1,0},{0,1},{3,2},{2,3},{5,4},{4,5},{7,6},{6,7},{9,8},{8,9},{11,10... | collective-permute-start | bytes 2359304 | tf_op jit(solution)/shard_map/ppermute | solution.py:35
  1248.9 29.9 %collective-permute-start.44 = (bf16[768,512]{1,0:T(8,128)(2,1)}, bf16[768,512]{1,0:T(8,128)(2,1)}, u32[]{:S(2)}, u32[]{:S(2)}) collective-permute-start(bf16[768,512]{1,0:T(8,128)(2,1)} %get-tuple-element.23), channel_id=1, source_target_pairs={{1,0},{0,1},{3,2},{2,3},{5,4},{4,5},{7,6},{6,7},{9,8},{8,9},{11,10... | collective-permute-start | bytes 2359304 | tf_op jit(solution)/shard_map/ppermute | solution.py:35
  1250.2 28.6 %collective-permute-start.48 = (bf16[768,512]{1,0:T(8,128)(2,1)}, bf16[768,512]{1,0:T(8,128)(2,1)}, u32[]{:S(2)}, u32[]{:S(2)}) collective-permute-start(bf16[768,512]{1,0:T(8,128)(2,1)} %get-tuple-element.24), channel_id=1, source_target_pairs={{2,0},{3,1},{0,2},{1,3},{6,4},{7,5},{4,6},{5,7},{10,8},{11,9},{8,1... | collective-permute-start | bytes 2359304 | tf_op jit(solution)/shard_map/ppermute | solution.py:35
  1255.3 32.6 %collective-permute-start.46 = (bf16[768,512]{1,0:T(8,128)(2,1)S(1)}, bf16[768,512]{1,0:T(8,128)(2,1)}, u32[]{:S(2)}, u32[]{:S(2)}) collective-permute-start(bf16[768,512]{1,0:T(8,128)(2,1)S(1)} %fusion.37), channel_id=1, source_target_pairs={{2,0},{3,1},{0,2},{1,3},{6,4},{7,5},{4,6},{5,7},{10,8},{11,9},{8,1... | collective-permute-start | bytes 2359304 | tf_op jit(solution)/shard_map/ppermute | solution.py:35
  1277.9 23.0 %collective-permute-start.47 = (bf16[768,512]{1,0:T(8,128)(2,1)S(1)}, bf16[768,512]{1,0:T(8,128)(2,1)S(1)}, u32[]{:S(2)}, u32[]{:S(2)}) collective-permute-start(bf16[768,512]{1,0:T(8,128)(2,1)S(1)} %get-tuple-element.25), channel_id=1, source_target_pairs={{2,0},{3,1},{0,2},{1,3},{6,4},{7,5},{4,6},{5,7},{10,8},{11,9},{8,1... | collective-permute-start | bytes 2359304 | tf_op jit(solution)/shard_map/ppermute | solution.py:35
  1290.7 12.1 collective-permute-start.49
  1312.4 65.9 %collective-permute-start.50 = (bf16[384,1024]{1,0:T(8,128)(2,1)}, bf16[384,1024]{1,0:T(8,128)(2,1)S(1)}, u32[]{:S(2)}, u32[]{:S(2)}) collective-permute-start(bf16[384,1024]{1,0:T(8,128)(2,1)} %get-tuple-element.58), channel_id=1, source_target_pairs={{1,0},{0,1},{3,2},{2,3},{5,4},{4,5},{7,6},{6,7},{9,8},{8,9},{11,10... | collective-permute-start | bytes 2359304 | tf_op jit(solution)/shard_map/ppermute | solution.py:35
  1313.1 67.5 %collective-permute-start.53 = (bf16[384,1024]{1,0:T(8,128)(2,1)}, bf16[384,1024]{1,0:T(8,128)(2,1)S(1)}, u32[]{:S(2)}, u32[]{:S(2)}) collective-permute-start(bf16[384,1024]{1,0:T(8,128)(2,1)} %get-tuple-element.57), channel_id=1, source_target_pairs={{2,0},{3,1},{0,2},{1,3},{6,4},{7,5},{4,6},{5,7},{10,8},{11,9},{8,1... | collective-permute-start | bytes 2359304 | tf_op jit(solution)/shard_map/ppermute | solution.py:35
  1317.2 65.1 %collective-permute-start.51 = (bf16[384,1024]{1,0:T(8,128)(2,1)}, bf16[384,1024]{1,0:T(8,128)(2,1)}, u32[]{:S(2)}, u32[]{:S(2)}) collective-permute-start(bf16[384,1024]{1,0:T(8,128)(2,1)} %get-tuple-element.57), channel_id=1, source_target_pairs={{1,0},{0,1},{3,2},{2,3},{5,4},{4,5},{7,6},{6,7},{9,8},{8,9},{11,10... | collective-permute-start | bytes 2359304 | tf_op jit(solution)/shard_map/ppermute | solution.py:35
  1318.6 65.7 %collective-permute-start.52 = (bf16[384,1024]{1,0:T(8,128)(2,1)}, bf16[384,1024]{1,0:T(8,128)(2,1)}, u32[]{:S(2)}, u32[]{:S(2)}) collective-permute-start(bf16[384,1024]{1,0:T(8,128)(2,1)} %get-tuple-element.58), channel_id=1, source_target_pairs={{2,0},{3,1},{0,2},{1,3},{6,4},{7,5},{4,6},{5,7},{10,8},{11,9},{8,1... | collective-permute-start | bytes 2359304 | tf_op jit(solution)/shard_map/ppermute | solution.py:35
  1378.3 18.9 %collective-permute-start.54 = (bf16[384,1024]{1,0:T(8,128)(2,1)S(1)}, bf16[384,1024]{1,0:T(8,128)(2,1)S(1)}, u32[]{:S(2)}, u32[]{:S(2)}) collective-permute-start(bf16[384,1024]{1,0:T(8,128)(2,1)S(1)} %collective-permute-done.50), channel_id=1, source_target_pairs={{2,0},{3,1},{0,2},{1,3},{6,4},{7,5},{4,6},{5,7},{10,8},{11,9},{8,1... | collective-permute-start | bytes 2359304 | tf_op jit(solution)/shard_map/ppermute | solution.py:35
  1380.6 17.5 %collective-permute-start.55 = (bf16[384,1024]{1,0:T(8,128)(2,1)S(1)}, bf16[384,1024]{1,0:T(8,128)(2,1)S(1)}, u32[]{:S(2)}, u32[]{:S(2)}) collective-permute-start(bf16[384,1024]{1,0:T(8,128)(2,1)S(1)} %collective-permute-done.53), channel_id=1, source_target_pairs={{1,0},{0,1},{3,2},{2,3},{5,4},{4,5},{7,6},{6,7},{9,8},{8,9},{11,10... | collective-permute-start | bytes 2359304 | tf_op jit(solution)/shard_map/ppermute | solution.py:35
  (73 other events, 2001.0 us)
Sparse Core Ops, SparseCore 0:
  117.6 50.9 all-gather.1
  1317.3 98.1 all-reduce.2
